TPU v7x, 256 devices: a whole 4x4x8 slice. The times are simulated.
256 devices in a mesh: tok: 64 (over z, x, core), head: 4 (over y).
Axes of the slice: x: 4, y: 4, z: 8, core: 2. Of those that a mesh axis runs over, the one named last changes fastest.
Arguments:
- single: bfloat16 [2048, 768], P('tok'), may hold values from -6 to 6
- pair: bfloat16 [2048, 2048, 128], P('tok', 'head'), may hold values from -161 to 161
- atoms: bfloat16 [49152, 128], P('tok'), may hold values from -60 to 60
- atom_counts: int32 [2048], P('tok'), may hold values from 4 to 24, as said below
- w_atom: bfloat16 [128, 3, 128], P(None, None, 'head'), may hold values from -0.5 to 0.5
- w_atom_token: bfloat16 [128, 768], P('head'), may hold values from -6 to 6
- ln_gain: bfloat16 [768], replicated, may hold values from 0.099609375 to 1.8984375
- w_proj: bfloat16 [768, 4, 768], P(None, None, 'head'), may hold values from -0.21875 to 0.21875
- w_pair_bias: bfloat16 [128, 16], replicated, may hold values from -3.5 to 3.5
- w_out: bfloat16 [768, 768], P('head'), may hold values from -0.21875 to 0.21875
- ln_gain2: bfloat16 [768], replicated, may hold values from 0.099609375 to 1.8984375
- w_trans: bfloat16 [768, 2, 1536], P(None, None, 'head'), may hold values from -0.21875 to 0.21875
- w_trans_out: bfloat16 [1536, 768], P('head'), may hold values from -0.15625 to 0.15625
Outputs:
- refined: bfloat16 [2048, 768], P('tok', 'head')
- atom_mix: bfloat16 [128, 49152], P('head', 'tok')
Inputs may be any that keep to these rules, and one draw needn't show every extreme that they name: `atom_counts`: every token has 4 to 24 atoms; in every draw all tokens of some group of 32 have 24 atoms.
All inputs are finite; a program needn't handle non-finite values.
Results may differ from a plain program's by a relative error of at most 0.013.
Values may be sent and summed in bfloat16 or wider, within the bound.
No kernel may reach another device: no remote copies, remote signals or barrier semaphores. Data moves between devices by JAX's collectives and lax.ppermute only.
A program may use at most 64 MiB of HBM per device.

v0:
```python
import jax
import jax.numpy as jnp
from jax import lax
from jax.sharding import PartitionSpec as P

H = 16
AH = 4
QWIN = 32
KWIN = 128


norm_eps = 1e-05
masked_value = -1000000000.0


def from_behind(block, axis, distance):
    devices = range(lax.axis_size(axis))
    route = [(i - distance, i) for i in devices if i - distance in devices]
    return lax.ppermute(block, axis, route)


def sent_to_all(value, axis):
    copies = jnp.broadcast_to(value, (lax.axis_size(axis), *value.shape))
    return lax.all_to_all(copies, axis, split_axis=0, concat_axis=0, tiled=True)


def of_everyone(value, axis):
    return sent_to_all(value, axis).astype(jnp.float32).sum(axis=0)


def joined_along(pieces, dim):
    pieces = jnp.moveaxis(pieces, 0, dim)
    dims = pieces.shape
    return pieces.reshape(*dims[:dim], dims[dim] * dims[dim + 1], *dims[dim + 2 :])


def gather_directly(value, axis, dim):
    return joined_along(sent_to_all(value, axis), dim)


def in_blocks(value, dim, size):
    before, after = (value.shape[:dim], value.shape[dim + 1 :])
    return jnp.moveaxis(value.reshape(*before, size, -1, *after), dim, 0)


def sum_at_owner(value, axis, dim):
    pieces = in_blocks(value, dim, lax.axis_size(axis))
    arrived = lax.all_to_all(pieces, axis, split_axis=0, concat_axis=0, tiled=True)
    return arrived.astype(jnp.float32).sum(axis=0)


def layer_norm(value_entries, gain):
    average = jnp.mean(value_entries, axis=-1, keepdims=True)
    centred = value_entries - average
    spread = jnp.mean(centred * centred, axis=-1, keepdims=True)
    return centred * lax.rsqrt(spread + norm_eps) * gain.astype(jnp.float32)


def atom_windows(atoms, atom_counts, w_atom):
    slot_count = atoms.shape[0]
    channels = atoms.shape[1]
    local_width = w_atom.shape[2]
    head_size = channels // AH
    local_heads = local_width // head_size
    tail_rows = (KWIN - QWIN) // 2
    head_rows = (KWIN + QWIN) // 2
    live_total = jnp.sum(atom_counts)
    device_pos = lax.axis_index("tok")
    device_last = lax.axis_size("tok") - 1
    tail_block = lax.dynamic_slice_in_dim(atoms, live_total - tail_rows, tail_rows, 0)
    previous = from_behind(tail_block, "tok", 1)
    following = from_behind(atoms[:head_rows], "tok", -1)
    extended = jnp.concatenate([atoms, jnp.zeros((head_rows, channels), atoms.dtype)], axis=0)
    extended = lax.dynamic_update_slice(extended, following, (live_total, jnp.int32(0)))
    keyed_rows = jnp.concatenate([previous, extended], axis=0)
    projected_rows = jnp.dot(
        keyed_rows, w_atom.reshape(channels, 3 * local_width), preferred_element_type=jnp.float32
    ).astype(jnp.bfloat16)
    windows = slot_count // QWIN
    queries = projected_rows[tail_rows : tail_rows + slot_count, :local_width].reshape(
        windows, QWIN, local_heads, head_size
    )
    blocked = projected_rows[:, local_width:].reshape(windows + KWIN // QWIN, QWIN, 2 * local_width)
    stacked = jnp.stack(
        [blocked[step_pos : step_pos + windows] for step_pos in range(KWIN // QWIN)], axis=1
    )
    stacked = stacked.reshape(windows, KWIN, 2, local_heads, head_size)
    key_rows = stacked[:, :, 0]
    value_rows = stacked[:, :, 1]
    scores = jnp.einsum(
        "wqhd,wkhd->whqk", queries, key_rows, preferred_element_type=jnp.float32
    ) * head_size ** (-0.5)
    window_pos = jnp.arange(windows, dtype=jnp.int32)
    key_pos = window_pos[:, None] * QWIN + jnp.arange(KWIN, dtype=jnp.int32)[None, :] - tail_rows
    key_valid = (
        (key_pos < 0) & (device_pos > 0)
        | (key_pos >= 0) & (key_pos < live_total)
        | (key_pos >= live_total) & (device_pos < device_last)
    )
    scores = jnp.where(key_valid[:, None, None, :], scores, masked_value)
    row_max = jnp.max(scores, axis=-1, keepdims=True)
    lifted = jnp.exp(scores - row_max)
    weights = (lifted / jnp.sum(lifted, axis=-1, keepdims=True)).astype(jnp.bfloat16)
    atom_out = jnp.einsum(
        "whqk,wkhd->wqhd", weights, value_rows, preferred_element_type=jnp.float32
    )
    query_live = (jnp.arange(slot_count, dtype=jnp.int32) < live_total).reshape(windows, QWIN)
    atom_out = jnp.where(query_live[:, :, None, None], atom_out, 0.0)
    return atom_out.reshape(slot_count, local_width).astype(jnp.bfloat16)


def token_means(atom_out, atom_counts):
    starts = jnp.cumsum(atom_counts) - atom_counts
    slot_position = jnp.arange(atom_out.shape[0], dtype=jnp.int32)
    member = (slot_position[None, :] >= starts[:, None]) & (
        slot_position[None, :] < (starts + atom_counts)[:, None]
    )
    totals_rows = jnp.dot(member.astype(jnp.bfloat16), atom_out, preferred_element_type=jnp.float32)
    return totals_rows / atom_counts[:, None].astype(jnp.float32)


def shards(
    single,
    pair,
    atoms,
    atom_counts,
    w_atom,
    w_atom_token,
    ln_gain,
    w_proj,
    w_pair_bias,
    w_out,
    ln_gain2,
    w_trans,
    w_trans_out,
):
    atom_out = atom_windows(atoms, atom_counts, w_atom)
    token_atoms = token_means(atom_out, atom_counts).astype(jnp.bfloat16)
    atom_part = jnp.dot(token_atoms, w_atom_token, preferred_element_type=jnp.float32)
    atom_term = of_everyone(atom_part.astype(jnp.bfloat16), "head").astype(jnp.float32)
    residual_state = single.astype(jnp.float32) + atom_term
    normed = layer_norm(residual_state, ln_gain).astype(jnp.bfloat16)
    model_width = single.shape[1]
    local_width = w_proj.shape[2]
    head_size = model_width // H
    local_heads = local_width // head_size
    row_count = normed.shape[0]
    flat_proj = w_proj.reshape(model_width, 4 * local_width)
    own_proj = jnp.dot(normed, flat_proj, preferred_element_type=jnp.float32)
    queries = own_proj[:, :local_width].astype(jnp.bfloat16)
    gate_raw = own_proj[:, 3 * local_width :]
    key_value = own_proj[:, local_width : 3 * local_width].astype(jnp.bfloat16)
    gathered = gather_directly(key_value, "tok", 0)
    token_count = gathered.shape[0]
    key_value_rows = gathered.reshape(token_count, 2, local_heads, head_size)
    pair_term = jnp.einsum(
        "ikc,ch->hik", pair, w_pair_bias, preferred_element_type=jnp.float32
    ).astype(jnp.bfloat16)
    pair_term = lax.all_to_all(pair_term, "head", split_axis=0, concat_axis=2, tiled=True)
    query_rows = queries.reshape(row_count, local_heads, head_size)
    scores = jnp.einsum(
        "qhd,khd->hqk", query_rows, key_value_rows[:, 0], preferred_element_type=jnp.float32
    ) * head_size ** (-0.5)
    scores = scores + pair_term.astype(jnp.float32)
    row_max = jnp.max(scores, axis=-1, keepdims=True)
    lifted = jnp.exp(scores - row_max)
    weights = (lifted / jnp.sum(lifted, axis=-1, keepdims=True)).astype(jnp.bfloat16)
    context = jnp.einsum(
        "hqk,khd->qhd", weights, key_value_rows[:, 1], preferred_element_type=jnp.float32
    )
    context = context.reshape(row_count, local_width)
    gated_rows = (context * jax.nn.sigmoid(gate_raw)).astype(jnp.bfloat16)
    mixing = jnp.dot(gated_rows, w_out, preferred_element_type=jnp.float32)
    quarter = model_width // lax.axis_size("head")
    offset = lax.axis_index("head") * quarter
    state_after = residual_state + of_everyone(mixing.astype(jnp.bfloat16), "head").astype(
        jnp.float32
    )
    own_share = lax.dynamic_slice_in_dim(state_after, offset, quarter, 1)
    normed_after = layer_norm(state_after, ln_gain2).astype(jnp.bfloat16)
    hidden_local = w_trans.shape[2]
    gate_up = jnp.dot(
        normed_after,
        w_trans.reshape(model_width, 2 * hidden_local),
        preferred_element_type=jnp.float32,
    )
    hidden = (jax.nn.silu(gate_up[:, :hidden_local]) * gate_up[:, hidden_local:]).astype(
        jnp.bfloat16
    )
    update = sum_at_owner(
        jnp.dot(hidden, w_trans_out, preferred_element_type=jnp.float32).astype(jnp.bfloat16),
        "head",
        1,
    )
    refined = (own_share + update).astype(jnp.bfloat16)
    return (refined, atom_out.T)


def solution(mesh):
    return jax.shard_map(
        shards,
        mesh=mesh,
        in_specs=(
            P("tok", None),
            P("tok", "head", None),
            P("tok", None),
            P("tok"),
            P(None, None, "head"),
            P("head", None),
            P(),
            P(None, None, "head"),
            P(),
            P("head", None),
            P(),
            P(None, None, "head"),
            P("head", None),
        ),
        out_specs=(P("tok", "head"), P("head", "tok")),
        check_vma=False,
    )
```

profile of v0, /device:TPU:6, one launch (start us, length us, event | category | flops | bytes accessed | tf_op | source)
XLA Modules:
  0.0 143.3 jit_solution(10837507547731607174)
XLA Ops:
  1.6 1.9 %fusion.67 = (f32[32]{0:T(128)S(1)}, s32[32]{0:T(128)}, s32[]{:T(128)}) fusion(s32[32]{0:T(128)} %param.16, s32[32]{0:T(128)S(1)} %reduce.4), kind=kLoop, calls=%fused_computation.98 | loop fusion | flops 95 | bytes 516 | tf_op jit(solution)/shard_map/convert_element_type | solution.py:119
  5.6 1.9 %collective-permute-start = (bf16[48,128]{1,0:T(8,128)(2,1)S(1)}, bf16[48,128]{1,0:T(8,128)(2,1)S(1)}, u32[]{:S(2)}, u32[]{:S(2)}) collective-permute-start(bf16[48,128]{1,0:T(8,128)(2,1)S(1)} %constant_dynamic-slice_fusion), channel_id=1, source_target_pairs={{0,4},{4,8},{8,12},{12,16},{16,20},{20,24},{24,28},{28,32},{32,36}... | collective-permute-start | bytes 36872 | tf_op jit(solution)/shard_map/ppermute | solution.py:19
  8.2 3.6 %collective-permute-start.1 = (bf16[80,128]{1,0:T(8,128)(2,1)S(1)}, bf16[80,128]{1,0:T(8,128)(2,1)S(1)}, u32[]{:S(2)}, u32[]{:S(2)}) collective-permute-start(bf16[80,128]{1,0:T(8,128)(2,1)S(1)} %slice.56), channel_id=1, source_target_pairs={{4,0},{8,4},{12,8},{16,12},{20,16},{24,20},{28,24},{32,28},{36,32}... | collective-permute-start | bytes 61448 | tf_op jit(solution)/shard_map/ppermute | solution.py:19
  21.7 1.4 fusion.10
  24.4 4.5 %all-to-all-start = ((bf16[4,32,768]{2,1,0:T(8,128)(2,1)}), bf16[4,32,768]{2,1,0:T(8,128)(2,1)S(1)}, u32[]{:S(2)}, u32[]{:S(2)}) async-start(bf16[4,32,768]{2,1,0:T(8,128)(2,1)} %broadcast_in_dim.34), calls=%async_computation | async-start | bytes 393216 | tf_op jit(solution)/shard_map/all_to_all | solution.py:24
  28.9 3.4 %convolution_convert_fusion = bf16[16,32,512]{2,0,1:T(8,128)(2,1)S(1)} fusion(bf16[32,512,128]{2,1,0:T(8,128)(2,1)} %param.14, bf16[128,16]{0,1:T(8,128)(2,1)S(1)} %copy-done.8), kind=kOutput, calls=%fused_computation.6 | convolution fusion | flops 67371008 | bytes 4722688 | tf_op jit(solution)/shard_map/ikc,ch->hik/dot_general | solution.py:156
  33.4 2.7 %all-to-all-done = bf16[4,32,768]{2,1,0:T(8,128)(2,1)S(1)} async-done(((bf16[4,32,768]{2,1,0:T(8,128)(2,1)}), bf16[4,32,768]{2,1,0:T(8,128)(2,1)S(1)}, u32[]{:S(2)}, u32[]{:S(2)}) %all-to-all-start) | async-done | bytes 196640 | tf_op jit(solution)/shard_map/all_to_all | solution.py:24
  36.1 3.5 %all-to-all-start.2 = ((bf16[16,32,512]{2,1,0:T(8,128)(2,1)}), bf16[16,32,512]{2,1,0:T(8,128)(2,1)S(1)}, u32[]{:S(2)}, u32[]{:S(2)}) async-start(bf16[16,32,512]{2,1,0:T(8,128)(2,1)} %copy.66), calls=%async_computation.2 | async-start | bytes 1048576 | tf_op jit(solution)/shard_map/all_to_all | solution.py:159
  41.2 8.3 %all-to-all-done.2 = bf16[16,32,512]{2,1,0:T(8,128)(2,1)S(1)} async-done(((bf16[16,32,512]{2,1,0:T(8,128)(2,1)}), bf16[16,32,512]{2,1,0:T(8,128)(2,1)S(1)}, u32[]{:S(2)}, u32[]{:S(2)}) %all-to-all-start.2) | async-done | bytes 524320 | tf_op jit(solution)/shard_map/all_to_all | solution.py:159
  50.8 10.0 %all-to-all-start.1 = ((bf16[64,32,384]{2,1,0:T(8,128)(2,1)}), bf16[64,32,384]{2,1,0:T(8,128)(2,1)S(1)}, u32[]{:S(2)}, u32[]{:S(2)}) async-start(bf16[64,32,384]{2,1,0:T(8,128)(2,1)} %broadcast_in_dim.35), calls=%async_computation.1 | async-start | bytes 3145728 | tf_op jit(solution)/shard_map/all_to_all | solution.py:24
  63.0 1.4 copy.80
  64.3 2.9 %reshape.182 = f32[4,32,2048]{2,1,0:T(8,128)} reshape(f32[4,32,4,512]{3,2,1,0:T(4,128)} %bitcast.71) | data formatting | bytes 2097152 | tf_op jit(solution)/shard_map/convert_element_type | solution.py:164
  67.3 33.6 %all-to-all-done.1 = bf16[64,32,384]{2,1,0:T(8,128)(2,1)S(1)} async-done(((bf16[64,32,384]{2,1,0:T(8,128)(2,1)}), bf16[64,32,384]{2,1,0:T(8,128)(2,1)S(1)}, u32[]{:S(2)}, u32[]{:S(2)}) %all-to-all-start.1) | async-done | bytes 1572896 | tf_op jit(solution)/shard_map/all_to_all | solution.py:24
  100.9 4.7 %reshape_reshape.3 = bf16[2048,2,4,48]{3,2,1,0:T(4,128)(2,1)} reshape(bf16[64,32,384]{2,1,0:T(8,128)(2,1)S(1)} %all-to-all-done.1) | data formatting | bytes 3145728 | tf_op jit(solution)/shard_map/reshape;reshape | solution.py:155
  105.6 4.0 %fusion.65 = (bf16[2048,1,4,48]{3,2,1,0:T(4,128)(2,1)}, bf16[2048,1,4,48]{3,2,1,0:T(4,128)(2,1)S(1)}) fusion(bf16[2048,2,4,48]{3,2,1,0:T(4,128)(2,1)} %reshape_reshape.3), kind=kLoop, calls=%fused_computation.96 | loop fusion | bytes 3145728 | tf_op jit(solution)/shard_map/slice | solution.py:162
  109.6 4.0 %copy.74 = bf16[2048,1,4,48]{0,3,2,1:T(8,128)(2,1)} copy(bf16[2048,1,4,48]{3,2,1,0:T(4,128)(2,1)} %get-tuple-element.4) | data formatting | bytes 1572864
  113.6 1.7 %fusion.4 = f32[4,32,2048]{2,1,0:T(8,128)S(1)} fusion(f32[4,32,2048]{2,1,0:T(8,128)} %reshape.182, bf16[2048,1,4,48]{0,3,2,1:T(8,128)(2,1)} %copy.74, bf16[32,4,48]{2,1,0:T(4,128)(2,1)S(1)} %reshape.178), kind=kOutput, calls=%fused_computation.5 | convolution fusion | flops 25690112 | bytes 2895872 | tf_op jit(solution)/shard_map/qhd,khd->hqk/dot_general | solution.py:161
  116.7 2.3 %copy.73 = bf16[2048,1,4,48]{0,3,2,1:T(8,128)(2,1)} copy(bf16[2048,1,4,48]{3,2,1,0:T(4,128)(2,1)S(1)} %get-tuple-element.5) | data formatting | bytes 1572864
  119.0 2.2 %convolution_bitcast_fusion.1 = f32[32,4,48]{2,0,1:T(8,128)S(1)} fusion(bf16[2048,1,4,48]{0,3,2,1:T(8,128)(2,1)} %copy.73, f32[4,32]{1,0:T(4,128)S(1)} %fusion.70, f32[4,32,2048]{2,1,0:T(8,128)} %copy-done.1), kind=kOutput, calls=%fused_computation.19 | convolution fusion | flops 25954432 | bytes 1860096 | tf_op jit(solution)/shard_map/hqk,khd->qhd/dot_general | solution.py:168
  122.4 3.4 %all-to-all-start.3 = ((bf16[4,32,768]{2,1,0:T(8,128)(2,1)}), bf16[4,32,768]{2,1,0:T(8,128)(2,1)S(1)}, u32[]{:S(2)}, u32[]{:S(2)}) async-start(bf16[4,32,768]{2,1,0:T(8,128)(2,1)} %broadcast_in_dim.36), calls=%async_computation.3 | async-start | bytes 393216 | tf_op jit(solution)/shard_map/all_to_all | solution.py:24
  125.7 1.5 %copy.75 = bf16[96,8,2,384]{3,1,2,0:T(8,128)(2,1)S(1)} copy(bf16[96,8,2,384]{3,2,1,0:T(2,128)(2,1)} %bitcast.73) | data formatting | bytes 2359296
  127.3 4.8 %all-to-all-done.3 = bf16[4,32,768]{2,1,0:T(8,128)(2,1)S(1)} async-done(((bf16[4,32,768]{2,1,0:T(8,128)(2,1)}), bf16[4,32,768]{2,1,0:T(8,128)(2,1)S(1)}, u32[]{:S(2)}, u32[]{:S(2)}) %all-to-all-start.3) | async-done | bytes 196640 | tf_op jit(solution)/shard_map/all_to_all | solution.py:24
  133.7 3.3 %all-to-all-start.4 = ((bf16[4,32,192]{2,1,0:T(8,128)(2,1)}), bf16[4,32,192]{2,1,0:T(8,128)(2,1)S(1)}, u32[]{:S(2)}, u32[]{:S(2)}) async-start(bf16[4,32,192]{2,1,0:T(8,128)(2,1)} %bitcast.68), calls=%async_computation.4 | async-start | bytes 131072 | tf_op jit(solution)/shard_map/all_to_all | solution.py:48
  137.0 5.6 %all-to-all-done.4 = bf16[4,32,192]{2,1,0:T(8,128)(2,1)S(1)} async-done(((bf16[4,32,192]{2,1,0:T(8,128)(2,1)}), bf16[4,32,192]{2,1,0:T(8,128)(2,1)S(1)}, u32[]{:S(2)}, u32[]{:S(2)}) %all-to-all-start.4) | async-done | bytes 49184 | tf_op jit(solution)/shard_map/all_to_all | solution.py:48
  (84 shorter events, 22.4 us)
Async XLA Ops:
  0.6 39.4 %copy-start = (bf16[768,4,192]{0,2,1:T(8,128)(2,1)S(1)}, bf16[768,4,192]{0,2,1:T(8,128)(2,1)}, u32[]{:S(2)}) copy-start(bf16[768,4,192]{0,2,1:T(8,128)(2,1)} %param.20) | copy-start | bytes 3538948
  5.6 10.9 %collective-permute-start = (bf16[48,128]{1,0:T(8,128)(2,1)S(1)}, bf16[48,128]{1,0:T(8,128)(2,1)S(1)}, u32[]{:S(2)}, u32[]{:S(2)}) collective-permute-start(bf16[48,128]{1,0:T(8,128)(2,1)S(1)} %constant_dynamic-slice_fusion), channel_id=1, source_target_pairs={{0,4},{4,8},{8,12},{12,16},{16,20},{20,24},{24,28},{28,32},{32,36}... | collective-permute-start | bytes 36872 | tf_op jit(solution)/shard_map/ppermute | solution.py:19
  8.2 7.9 %collective-permute-start.1 = (bf16[80,128]{1,0:T(8,128)(2,1)S(1)}, bf16[80,128]{1,0:T(8,128)(2,1)S(1)}, u32[]{:S(2)}, u32[]{:S(2)}) collective-permute-start(bf16[80,128]{1,0:T(8,128)(2,1)S(1)} %slice.56), channel_id=1, source_target_pairs={{4,0},{8,4},{12,8},{16,12},{20,16},{24,20},{28,24},{32,28},{36,32}... | collective-permute-start | bytes 61448 | tf_op jit(solution)/shard_map/ppermute | solution.py:19
  20.2 0.8 copy-start.5
  21.4 2.0 %copy-start.11 = (s32[32]{0:T(128)S(1)}, s32[32]{0:T(128)}, u32[]{:S(2)}) copy-start(s32[32]{0:T(128)} %get-tuple-element.11) | copy-start | bytes 388
  21.4 2.0 %copy-start.12 = (bf16[32,768]{1,0:T(8,128)(2,1)S(1)}, bf16[32,768]{1,0:T(8,128)(2,1)}, u32[]{:S(2)}) copy-start(bf16[32,768]{1,0:T(8,128)(2,1)} %param.18) | copy-start | bytes 147460
  21.7 7.2 %copy-start.8 = (bf16[128,16]{0,1:T(8,128)(2,1)S(1)}, bf16[128,16]{0,1:T(8,128)(2,1)}, u32[]{:S(2)}) copy-start(bf16[128,16]{0,1:T(8,128)(2,1)} %param.21) | copy-start | bytes 12292
  23.3 8.9 %copy-start.7 = (bf16[768,32]{0,1:T(8,128)(2,1)}, bf16[768,32]{0,1:T(8,128)(2,1)S(1)}, u32[]{:S(2)}) copy-start(bf16[768,32]{0,1:T(8,128)(2,1)S(1)} %convert_element_type.91) | copy-start | bytes 147460
  24.4 11.7 %all-to-all-start = ((bf16[4,32,768]{2,1,0:T(8,128)(2,1)}), bf16[4,32,768]{2,1,0:T(8,128)(2,1)S(1)}, u32[]{:S(2)}, u32[]{:S(2)}) async-start(bf16[4,32,768]{2,1,0:T(8,128)(2,1)} %broadcast_in_dim.34), calls=%async_computation | async-start | bytes 393216 | tf_op jit(solution)/shard_map/all_to_all | solution.py:24
  28.9 3.4 %copy-start.9 = (bf16[768]{0:T(1024)(128)(2,1)S(1)}, bf16[768]{0:T(1024)(128)(2,1)}, u32[]{:S(2)}) copy-start(bf16[768]{0:T(1024)(128)(2,1)} %param.19) | copy-start | bytes 4612
  32.3 7.4 %copy-start.2 = (bf16[32,768]{1,0:T(8,128)(2,1)S(1)}, bf16[32,768]{1,0:T(8,128)(2,1)}, u32[]{:S(2)}) copy-start(bf16[32,768]{1,0:T(8,128)(2,1)} %param.13) | copy-start | bytes 147460
  36.1 13.4 %all-to-all-start.2 = ((bf16[16,32,512]{2,1,0:T(8,128)(2,1)}), bf16[16,32,512]{2,1,0:T(8,128)(2,1)S(1)}, u32[]{:S(2)}, u32[]{:S(2)}) async-start(bf16[16,32,512]{2,1,0:T(8,128)(2,1)} %copy.66), calls=%async_computation.2 | async-start | bytes 1048576 | tf_op jit(solution)/shard_map/all_to_all | solution.py:159
  40.5 0.6 copy-start.6
  50.8 50.1 %all-to-all-start.1 = ((bf16[64,32,384]{2,1,0:T(8,128)(2,1)}), bf16[64,32,384]{2,1,0:T(8,128)(2,1)S(1)}, u32[]{:S(2)}, u32[]{:S(2)}) async-start(bf16[64,32,384]{2,1,0:T(8,128)(2,1)} %broadcast_in_dim.35), calls=%async_computation.1 | async-start | bytes 3145728 | tf_op jit(solution)/shard_map/all_to_all | solution.py:24
  115.4 1.0 copy-start.1
  119.0 2.4 %copy-start.4 = (bf16[192,768]{1,0:T(8,128)(2,1)S(1)}, bf16[192,768]{1,0:T(8,128)(2,1)}, u32[]{:S(2)}) copy-start(bf16[192,768]{1,0:T(8,128)(2,1)} %param.22) | copy-start | bytes 884740
  121.7 5.6 %copy-start.10 = (bf16[768]{0:T(1024)(128)(2,1)S(1)}, bf16[768]{0:T(1024)(128)(2,1)}, u32[]{:S(2)}) copy-start(bf16[768]{0:T(1024)(128)(2,1)} %param.23) | copy-start | bytes 4612
  122.4 9.7 %all-to-all-start.3 = ((bf16[4,32,768]{2,1,0:T(8,128)(2,1)}), bf16[4,32,768]{2,1,0:T(8,128)(2,1)S(1)}, u32[]{:S(2)}, u32[]{:S(2)}) async-start(bf16[4,32,768]{2,1,0:T(8,128)(2,1)} %broadcast_in_dim.36), calls=%async_computation.3 | async-start | bytes 393216 | tf_op jit(solution)/shard_map/all_to_all | solution.py:24
  127.3 5.5 %copy-start.3 = (bf16[384,768]{1,0:T(8,128)(2,1)S(1)}, bf16[384,768]{1,0:T(8,128)(2,1)}, u32[]{:S(2)}) copy-start(bf16[384,768]{1,0:T(8,128)(2,1)} %param.25) | copy-start | bytes 1769476
  133.7 8.9 %all-to-all-start.4 = ((bf16[4,32,192]{2,1,0:T(8,128)(2,1)}), bf16[4,32,192]{2,1,0:T(8,128)(2,1)S(1)}, u32[]{:S(2)}, u32[]{:S(2)}) async-start(bf16[4,32,192]{2,1,0:T(8,128)(2,1)} %bitcast.68), calls=%async_computation.4 | async-start | bytes 131072 | tf_op jit(solution)/shard_map/all_to_all | solution.py:48
where the time goes:
time: 145 us; the launch traced here: 143 us
  waiting for transfers between devices  55 us (38%)
  local copies, waits for them, and re-layouts  36.7 us (25%)
  starting transfers between devices  30.2 us (21%)
  matrix products  11.5 us (8%)
  other arithmetic  5.67 us (4%)
  between operations  4.3 us (3%)
    all_to_all x3, waiting for transfers between devices, sent_to_all(): return lax.all_to_all(copies, axis, split_axis=0, concat_axis=0, tiled=True)  41.1 us
    all_to_all x3, starting transfers between devices, sent_to_all(): return lax.all_to_all(copies, axis, split_axis=0, concat_axis=0, tiled=True)  17.9 us
    unnamed x29, local copies, waits for them, and re-layouts  9.59 us
    all_to_all x1, waiting for transfers between devices, shards(): lax.all_to_all(pair_term, 'head', split_axis=0, concat_axis=2, tiled=True)  8.31 us
    all_to_all x1, waiting for transfers between devices, sum_at_owner(): lax.all_to_all(pieces, axis, split_axis=0, concat_axis=0, tiled=True)  5.58 us
    ppermute x2, starting transfers between devices, from_behind(): return lax.ppermute(block, axis, route)  5.54 us
    another operation x1, local copies, waits for them, and re-layouts, shards(): key_value_rows = gathered.reshape(token_count, 2, local_heads, head_size)  4.66 us
    convert_element_type x2, local copies, waits for them, and re-layouts, shards(): scores = scores + pair_term.astype(jnp.float32)  4.32 us
  transfers between devices with their start and end apart: 7, of which 5 were waited for; matrix products, arithmetic and copies ran while one was open for 12% of the time, Pallas kernels for 0%

commit v1 on v0

v1 whole, which is shorter than its diff:
```python
import jax
import jax.numpy as jnp
from jax import lax
from jax.experimental import pallas as pl
from jax.experimental.pallas import tpu as pltpu
from jax.sharding import Mesh
from jax.sharding import PartitionSpec as P

H = 16
AH = 4
QWIN = 32
KWIN = 128
TAIL = (KWIN - QWIN) // 2
HEADROWS = (KWIN + QWIN) // 2
QBLOCK = 128
KBLOCK = QBLOCK + KWIN

norm_eps = 1e-05
masked_value = -1000000000.0
f32 = jnp.float32
bf16 = jnp.bfloat16
NT = (((1,), (1,)), ((), ()))
TOK = ("z", "x", "core")


def sent_around(block, axis, distance):
    size = lax.axis_size(axis)
    return lax.ppermute(block, axis, [(i, (i + distance) % size) for i in range(size)])


def from_behind(block, axis, distance):
    devices = range(lax.axis_size(axis))
    route = [(i - distance, i) for i in devices if i - distance in devices]
    return lax.ppermute(block, axis, route)


def of_everyone(partial):
    return [partial] + [sent_around(partial, "head", d) for d in (1, 2, 3)]


def exchanged(pieces, axis):
    return lax.all_to_all(pieces, axis, split_axis=0, concat_axis=0, tiled=True)


def live_atoms(count_ref):
    live = count_ref[0]
    for i in range(1, count_ref.shape[0]):
        live = live + count_ref[i]
    return live


def layer_norm(value, gain):
    average = jnp.mean(value, axis=-1, keepdims=True)
    centred = value - average
    spread = jnp.mean(centred * centred, axis=-1, keepdims=True)
    return centred * lax.rsqrt(spread + norm_eps) * gain


def halo_kernel(count_ref, atoms, head_rows, tail_rows, rows):
    live = live_atoms(count_ref)
    rows[...] = atoms[...].astype(f32)
    head_rows[...] = atoms[0:HEADROWS]
    tail_rows[...] = rows[pl.ds(live - TAIL, TAIL), :].astype(bf16)


def pair_kernel(pair, w_bias, out):
    half = pair.shape[1] // 2
    w = w_bias[...].astype(f32)
    blank = jnp.zeros_like(w)
    both = jnp.concatenate(
        [jnp.concatenate([w, blank], axis=1), jnp.concatenate([blank, w], axis=1)], axis=0
    ).astype(bf16)
    terms = []
    for q in range(pair.shape[0]):
        keys = jnp.concatenate([pair[q, :half], pair[q, half:]], axis=1)
        term = lax.dot_general(both, keys, NT, preferred_element_type=f32)
        terms.append(jnp.concatenate([term[:H], term[H:]], axis=1))
    out[...] = jnp.stack(terms, axis=1).astype(bf16)


def atom_kernel(
    where_ref, count_ref, counts_row, atoms, previous, following, w_atom, w_token, partial, mix, rows
):
    slots = atoms.shape[0]
    tokens = counts_row.shape[1]
    width = w_token.shape[0]
    live = live_atoms(count_ref)
    first = where_ref[0] == 0
    last = where_ref[0] == where_ref[1]
    rows[0:TAIL] = previous[...].astype(f32)
    rows[TAIL : TAIL + slots] = atoms[...].astype(f32)
    rows[TAIL + slots :] = jnp.zeros((HEADROWS, atoms.shape[1]), f32)
    rows[pl.ds(TAIL + live, HEADROWS), :] = following[...].astype(f32)
    keyed = rows[...].astype(bf16)

    def projected(part):
        w = w_atom[part * width : (part + 1) * width, :]
        return lax.dot_general(keyed, w, NT, preferred_element_type=f32)

    queries = projected(0)[TAIL : TAIL + slots].astype(bf16)
    keys = projected(1).astype(bf16)
    values = projected(2).astype(bf16)

    counts = jnp.broadcast_to(counts_row[...].astype(f32), (tokens, tokens))
    token_row = lax.broadcasted_iota(jnp.int32, (tokens, tokens), 0)
    token_lane = lax.broadcasted_iota(jnp.int32, (tokens, tokens), 1)
    starts = jnp.sum(jnp.where(token_lane < token_row, counts, 0.0), axis=1, keepdims=True)
    own = jnp.sum(jnp.where(token_lane == token_row, counts, 0.0), axis=1, keepdims=True)

    row = lax.broadcasted_iota(jnp.int32, (QBLOCK, KBLOCK), 0)
    lane = lax.broadcasted_iota(jnp.int32, (QBLOCK, KBLOCK), 1)
    offset = lane - (row // QWIN) * QWIN
    in_window = (offset >= 0) & (offset < KWIN)
    low = jnp.where(first, 0, -slots)
    high = jnp.where(last, live, 4 * slots)
    out_row = lax.broadcasted_iota(jnp.int32, (QBLOCK, width), 0)
    slot = lax.broadcasted_iota(jnp.int32, (tokens, QBLOCK), 1).astype(f32)
    totals = jnp.zeros((tokens, width), f32)
    for b in range(slots // QBLOCK):
        at = b * QBLOCK
        scores = lax.dot_general(
            queries[at : at + QBLOCK], keys[at : at + KBLOCK], NT, preferred_element_type=f32
        ) * width ** (-0.5)
        key_pos = lane + (at - TAIL)
        scores = jnp.where(in_window & (key_pos >= low) & (key_pos < high), scores, masked_value)
        lifted = jnp.exp(scores - jnp.max(scores, axis=1, keepdims=True))
        weights = (lifted / jnp.sum(lifted, axis=1, keepdims=True)).astype(bf16)
        out = jnp.dot(weights, values[at : at + KBLOCK], preferred_element_type=f32)
        out = jnp.where(out_row + at < live, out, 0.0)
        mix[:, at : at + QBLOCK] = out.T.astype(bf16)
        member = (slot + at >= starts) & (slot + at < starts + own)
        totals = totals + jnp.dot(
            jnp.where(member, 1.0, 0.0).astype(bf16), out.astype(bf16), preferred_element_type=f32
        )
    token_atoms = (totals / own).astype(bf16)
    partial[...] = jnp.dot(token_atoms, w_token[...], preferred_element_type=f32).astype(bf16)


def projection_kernel(p0, p1, p2, p3, single, gain, w_proj, residual, kv, query, gate):
    term = (p0[...].astype(f32) + p1[...].astype(f32)) + (p2[...].astype(f32) + p3[...].astype(f32))
    state = single[...].astype(f32) + term
    residual[...] = state
    normed = layer_norm(state, gain[...].astype(f32)).astype(bf16)
    own = lax.dot_general(normed, w_proj[...], NT, preferred_element_type=f32)
    part = own.shape[1] // 4
    query[...] = own[:, :part].astype(bf16)
    gate[...] = own[:, 3 * part :]
    pair = jnp.concatenate([own[:, 2 * part : 3 * part], own[:, part : 2 * part]], axis=1).astype(bf16)
    for i in range(kv.shape[0]):
        kv[i] = pair


def attention_kernel(where_ref, kv_own, kv_other, query, gate, bias, w_out, partial, kv, scores):
    core = where_ref[2]
    groups, tokens, width = kv_own.shape
    kv[:, pl.ds(core, 1)] = kv_own[...].reshape(groups, 1, tokens, width)
    kv[:, pl.ds(1 - core, 1)] = kv_other[...].reshape(groups, 1, tokens, width)
    part = query.shape[1]
    size = part // 4
    rows = 4 * tokens
    reach = 256
    blank = jnp.zeros((tokens, reach - part), f32)
    spread = jnp.concatenate([blank, query[...].astype(f32)], axis=1)
    spread = jnp.concatenate([spread] * 4, axis=0)
    head = lax.broadcasted_iota(jnp.int32, (rows, reach), 0) // tokens
    lane = lax.broadcasted_iota(jnp.int32, (rows, reach), 1) - (reach - part)
    queries = jnp.where((lane >= head * size) & (lane < (head + 1) * size), spread, 0.0)
    queries = queries.astype(bf16)
    keyed = kv[...].reshape(groups * 2 * tokens, width)
    block = bias.shape[2]
    scale = size ** (-0.5)
    top = None
    for b in range(4):
        s = lax.dot_general(
            queries,
            keyed[b * block : (b + 1) * block, width - reach :],
            NT,
            preferred_element_type=f32,
        ) * scale + bias[4 * b : 4 * b + 4].reshape(rows, block).astype(f32)
        scores[b] = s
        m = jnp.max(s, axis=1, keepdims=True)
        top = m if top is None else jnp.maximum(top, m)
    total = jnp.zeros((rows, 1), f32)
    context = jnp.zeros((rows, part), f32)
    for b in range(4):
        lifted = jnp.exp(scores[b] - top)
        total = total + jnp.sum(lifted, axis=1, keepdims=True)
        context = context + jnp.dot(
            lifted.astype(bf16),
            keyed[b * block : (b + 1) * block, :part],
            preferred_element_type=f32,
        )
    head = lax.broadcasted_iota(jnp.int32, (rows, part), 0) // tokens
    lane = lax.broadcasted_iota(jnp.int32, (rows, part), 1)
    own = (lane >= head * size) & (lane < (head + 1) * size)
    context = jnp.where(own, context / total, 0.0)
    mixed = sum(context[j * tokens : (j + 1) * tokens] for j in range(4))
    gated = (mixed * jax.nn.sigmoid(gate[...])).astype(bf16)
    partial[...] = jnp.dot(gated, w_out[...], preferred_element_type=f32).astype(bf16)


def tail_kernel(
    where_ref, p0, p1, p2, p3, residual, gain, w_trans, w_down, share, update, state
):
    term = (p0[...].astype(f32) + p1[...].astype(f32)) + (p2[...].astype(f32) + p3[...].astype(f32))
    after = residual[...] + term
    quarter = share.shape[1]
    for y in range(4):
        state[y] = after[:, y * quarter : (y + 1) * quarter]
    share[...] = state[where_ref[3]]
    normed = layer_norm(after, gain[...].astype(f32)).astype(bf16)
    gate = jnp.dot(normed, w_trans[0], preferred_element_type=f32)
    up = jnp.dot(normed, w_trans[1], preferred_element_type=f32)
    hidden = (gate * jax.nn.sigmoid(gate) * up).astype(bf16)
    moved = jnp.dot(hidden, w_down[...], preferred_element_type=f32)
    for y in range(4):
        update[y] = moved[:, y * quarter : (y + 1) * quarter].astype(bf16)


def call(kernel, out_shape, operands, scratch, smem):
    vmem = pl.BlockSpec(memory_space=pltpu.VMEM)
    scalar = pl.BlockSpec(memory_space=pltpu.SMEM)
    return pl.pallas_call(
        kernel,
        out_shape=out_shape,
        in_specs=[scalar] * smem + [vmem] * (len(operands) - smem),
        out_specs=jax.tree.map(lambda _: vmem, out_shape),
        scratch_shapes=scratch,
        compiler_params=pltpu.CompilerParams(vmem_limit_bytes=40 << 20),
        cost_estimate=pl.CostEstimate(flops=1 << 30, bytes_accessed=4 << 20, transcendentals=0),
    )(*operands)


def shards(
    single,
    pair,
    atoms,
    atom_counts,
    w_atom,
    w_atom_token,
    ln_gain,
    w_proj,
    w_pair_bias,
    w_out,
    ln_gain2,
    w_trans,
    w_trans_out,
):
    slots, channels = atoms.shape
    tokens, model = single.shape
    where_at = jnp.stack(
        [
            lax.axis_index(TOK),
            jnp.int32(lax.axis_size(TOK) - 1),
            lax.axis_index("core"),
            lax.axis_index("head"),
        ]
    ).astype(jnp.int32)
    head_rows, tail_rows = call(
        halo_kernel,
        (
            jax.ShapeDtypeStruct((HEADROWS, channels), bf16),
            jax.ShapeDtypeStruct((TAIL, channels), bf16),
        ),
        (atom_counts, atoms),
        [pltpu.VMEM((slots, channels), f32)],
        1,
    )
    pair, head_rows, tail_rows = lax.optimization_barrier((pair, head_rows, tail_rows))
    following = from_behind(head_rows, TOK, -1)
    previous = from_behind(tail_rows, TOK, 1)

    keys = pair.shape[1]
    pair_term = pl.pallas_call(
        pair_kernel,
        out_shape=jax.ShapeDtypeStruct((H, tokens, keys), bf16),
        grid=(4,),
        in_specs=[
            pl.BlockSpec((tokens // 4, keys, pair.shape[2]), lambda i: (i, 0, 0)),
            pl.BlockSpec((H, pair.shape[2]), lambda i: (0, 0)),
        ],
        out_specs=pl.BlockSpec((H, tokens // 4, keys), lambda i: (0, i, 0)),
        cost_estimate=pl.CostEstimate(flops=2 << 30, bytes_accessed=8 << 20, transcendentals=0),
    )(pair, w_pair_bias.T)
    pair_term, previous, following = lax.optimization_barrier((pair_term, previous, following))
    bias = exchanged(pair_term, "head")

    width = w_atom.shape[2]
    partial, mix = call(
        atom_kernel,
        (
            jax.ShapeDtypeStruct((tokens, model), bf16),
            jax.ShapeDtypeStruct((width, slots), bf16),
        ),
        (
            where_at,
            atom_counts,
            atom_counts.reshape(1, tokens),
            atoms,
            previous,
            following,
            w_atom.transpose(1, 2, 0).reshape(3 * width, channels),
            w_atom_token,
        ),
        [pltpu.VMEM((TAIL + slots + HEADROWS, channels), f32)],
        2,
    )
    quarter = model // 4
    residual, kv, query, gate = call(
        projection_kernel,
        (
            jax.ShapeDtypeStruct((tokens, model), f32),
            jax.ShapeDtypeStruct((32, tokens, 2 * quarter), bf16),
            jax.ShapeDtypeStruct((tokens, quarter), bf16),
            jax.ShapeDtypeStruct((tokens, quarter), f32),
        ),
        (
            *of_everyone(partial),
            single,
            ln_gain.reshape(1, model),
            w_proj.transpose(1, 2, 0).reshape(-1, model),
        ),
        [],
        0,
    )
    kv, bias = lax.optimization_barrier((kv, bias))
    kv_own = exchanged(kv, ("z", "x"))
    kv_other = sent_around(kv_own, "core", 1)
    partial = call(
        attention_kernel,
        jax.ShapeDtypeStruct((tokens, model), bf16),
        (where_at, kv_own, kv_other, query, gate, bias, w_out),
        [
            pltpu.VMEM((32, 2, tokens, 2 * quarter), bf16),
            pltpu.VMEM((4, 4 * tokens, bias.shape[2]), f32),
        ],
        1,
    )
    share, update = call(
        tail_kernel,
        (
            jax.ShapeDtypeStruct((tokens, quarter), f32),
            jax.ShapeDtypeStruct((4, tokens, quarter), bf16),
        ),
        (
            where_at,
            *of_everyone(partial),
            residual,
            ln_gain2.reshape(1, model),
            w_trans.transpose(1, 0, 2),
            w_trans_out,
        ),
        [pltpu.VMEM((4, tokens, quarter), f32)],
        1,
    )
    update = exchanged(update, "head")
    refined = (share + update.astype(f32).sum(axis=0)).astype(bf16)
    return (refined, mix)


def solution(mesh):
    devices = mesh.devices.reshape(8, 4, 2, 4)
    return jax.shard_map(
        shards,
        mesh=Mesh(devices, ("z", "x", "core", "head")),
        in_specs=(
            P(TOK, None),
            P(TOK, "head", None),
            P(TOK, None),
            P(TOK),
            P(None, None, "head"),
            P("head", None),
            P(),
            P(None, None, "head"),
            P(),
            P("head", None),
            P(),
            P(None, None, "head"),
            P("head", None),
        ),
        out_specs=(P(TOK, "head"), P("head", TOK)),
        check_vma=False,
    )
```

time: 145 us -> 87.1 us (0.60)
  waiting for transfers between devices: 55 us -> 8.53 us
  blocking collectives: 0 us -> 43.1 us
  local copies, waits for them, and re-layouts: 36.7 us -> 1.8 us
  Pallas kernels: 0 us -> 12.4 us
  matrix products: 11.5 us -> 0 us
  starting transfers between devices: 30.2 us -> 19.3 us
  other arithmetic: 5.67 us -> 0.7 us
  between operations: 4.3 us -> 0.81 us
    all_to_all x5 -> x1, waiting for transfers between devices: 55 us -> 0.01 us  [exchanged(): return lax.all_to_all(pieces, axis, split_axis=0, concat_axis=0, tiled=True)]
    all_to_all x0 -> x2, blocking collectives: none -> 43.1 us  [exchanged(): return lax.all_to_all(pieces, axis, split_axis=0, concat_axis=0, tiled=True)]
    all_to_all x5 -> x1, starting transfers between devices: 24.6 us -> 4.48 us  [exchanged(): return lax.all_to_all(pieces, axis, split_axis=0, concat_axis=0, tiled=True)]
    pallas_call x0 -> x6, Pallas kernels: none -> 12.4 us  [the longest x5 7.48 us: call(): pl.pallas_call(kernel, out_shape=out_shape, in_specs=[scalar] * smem + [v...]
    dot_general x11 -> x0, matrix products: 11.5 us -> none  [the longest x1 3.39 us: shards(): jnp.einsum('ikc,ch->hik', pair, w_pair_bias, preferred_element_type=jnp.f...]
    ppermute x0 -> x7, starting transfers between devices: none -> 10.5 us  [sent_around(): lax.ppermute(block, axis, [(i, (i + distance) % size) for i in range(size)])]
    ppermute x0 -> x7, waiting for transfers between devices: none -> 8.52 us  [sent_around(): lax.ppermute(block, axis, [(i, (i + distance) % size) for i in range(size)])]
    unnamed x29 -> x27, local copies, waits for them, and re-layouts: 9.59 us -> 1.79 us
  transfers between devices with their start and end apart: 7 -> 10, of which waited for: 5 -> 7; matrix products, arithmetic and copies ran while one was open for 12% -> 0% of each run, Pallas kernels for 0% -> 10%
where the time goes in v1:
time: 87.1 us; the launch traced here: 86.6 us
  blocking collectives  43.1 us (49%)
  starting transfers between devices  19.3 us (22%)
  Pallas kernels  12.4 us (14%)
  waiting for transfers between devices  8.53 us (10%)
  local copies, waits for them, and re-layouts  1.8 us (2%)
    all_to_all x2, blocking collectives, exchanged(): return lax.all_to_all(pieces, axis, split_axis=0, concat_axis=0, tiled=True)  43.1 us
    ppermute x7, starting transfers between devices, sent_around(): lax.ppermute(block, axis, [(i, (i + distance) % size) for i in range(size)])  10.5 us
    ppermute x7, waiting for transfers between devices, sent_around(): lax.ppermute(block, axis, [(i, (i + distance) % size) for i in range(size)])  8.52 us
    pallas_call x5, Pallas kernels, call(): pl.pallas_call(kernel, out_shape=out_shape, in_specs=[scalar] * smem + [v...  7.48 us
    pallas_call x1, Pallas kernels, shards(): pl.pallas_call(pair_kernel, out_shape=jax.ShapeDtypeStruct((H, tokens, ke...  4.91 us
    all_to_all x1, starting transfers between devices, exchanged(): return lax.all_to_all(pieces, axis, split_axis=0, concat_axis=0, tiled=True)  4.48 us
    ppermute x2, starting transfers between devices, from_behind(): return lax.ppermute(block, axis, route)  4.33 us
    unnamed x27, local copies, waits for them, and re-layouts  1.79 us
  transfers between devices with their start and end apart: 10, of which 7 were waited for; matrix products, arithmetic and copies ran while one was open for 0% of the time, Pallas kernels for 10%

profile of v1, /device:TPU:6, one launch (start us, length us, event | category | flops | bytes accessed | tf_op | source)
XLA Modules:
  0.0 86.6 jit_solution(5527504863436702703)
XLA Ops:
  0.6 0.9 %copy-done.3 = bf16[768,128]{1,0:T(8,128)(2,1)S(1)} copy-done((bf16[768,128]{1,0:T(8,128)(2,1)S(1)}, bf16[768,128]{1,0:T(8,128)(2,1)}, u32[]{:S(2)}) %copy-start.3) | copy-done | bytes 196632
  1.6 0.7 copy-done.8
  2.2 0.6 shard_map.140
  2.8 2.2 %collective-permute-start.1 = (bf16[80,128]{1,0:T(8,128)(2,1)S(1)}, bf16[80,128]{1,0:T(8,128)(2,1)S(1)}, u32[]{:S(2)}, u32[]{:S(2)}) collective-permute-start(bf16[80,128]{1,0:T(8,128)(2,1)S(1)} %get-tuple-element.24), channel_id=1, source_target_pairs={{4,0},{8,4},{12,8},{16,12},{20,16},{24,20},{28,24},{32,28},{36,32}... | collective-permute-start | bytes 61448 | tf_op jit(solution)/shard_map/ppermute | solution.py:34
  5.0 2.2 %collective-permute-start = (bf16[48,128]{1,0:T(8,128)(2,1)S(1)}, bf16[48,128]{1,0:T(8,128)(2,1)S(1)}, u32[]{:S(2)}, u32[]{:S(2)}) collective-permute-start(bf16[48,128]{1,0:T(8,128)(2,1)S(1)} %get-tuple-element.23), channel_id=1, source_target_pairs={{0,4},{4,8},{8,12},{12,16},{16,20},{20,24},{24,28},{28,32},{32,36}... | collective-permute-start | bytes 36872 | tf_op jit(solution)/shard_map/ppermute | solution.py:34
  7.2 4.9 %shard_map.141 = bf16[16,32,512]{2,1,0:T(8,128)(2,1)} custom-call(bf16[32,512,128]{2,1,0:T(8,128)(2,1)} %pair, bf16[16,128]{1,0:T(8,128)(2,1)} %bitcast.18), custom_call_target="tpu_custom_call" | custom-call | flops 2147483648 | bytes 8388608 | tf_op jit(solution)/shard_map/pallas_call | solution.py:274
  12.1 4.5 %all-to-all-start = ((bf16[16,32,512]{2,1,0:T(8,128)(2,1)}), bf16[16,32,512]{2,1,0:T(8,128)(2,1)S(1)}, u32[]{:S(2)}, u32[]{:S(2)}) async-start(bf16[16,32,512]{2,1,0:T(8,128)(2,1)} %shard_map.141), calls=%async_computation | async-start | bytes 1048576 | tf_op jit(solution)/shard_map/all_to_all | solution.py:42
  16.7 3.1 %shard_map.142 = (bf16[32,768]{1,0:T(8,128)(2,1)S(1)}, bf16[32,768]{1,0:T(8,128)(2,1)}) custom-call(s32[4]{0:T(128)S(1)} %pad_add_fusion.where_ref, s32[32]{0:T(128)S(1)} %copy-done.9, s32[1,32]{1,0:T(1,128)S(1)} %bitcast.17, bf16[768,128]{1,0:T(8,128)(2,1)S(1)} %copy-done.4, bf16[48,128]{1,0:T(8,128)(2,1)S(1)} %collective-permute-done.previous, ...), custom_call_target="tpu_custom_call" | custom-call | flops 1073741824 | bytes 4194304 | tf_op jit(solution)/shard_map/pallas_call | solution.py:223
  19.8 2.0 %collective-permute-start.2 = (bf16[32,768]{1,0:T(8,128)(2,1)S(1)}, bf16[32,768]{1,0:T(8,128)(2,1)S(1)}, u32[]{:S(2)}, u32[]{:S(2)}) collective-permute-start(bf16[32,768]{1,0:T(8,128)(2,1)S(1)} %get-tuple-element.27.p0), channel_id=1, source_target_pairs={{0,1},{1,2},{2,3},{3,0},{4,5},{5,6},{6,7},{7,4},{8,9},{9,10},{10,1... | collective-permute-start | bytes 147464 | tf_op jit(solution)/shard_map/ppermute | solution.py:28
  21.8 2.7 %collective-permute-start.3 = (bf16[32,768]{1,0:T(8,128)(2,1)S(1)}, bf16[32,768]{1,0:T(8,128)(2,1)S(1)}, u32[]{:S(2)}, u32[]{:S(2)}) collective-permute-start(bf16[32,768]{1,0:T(8,128)(2,1)S(1)} %get-tuple-element.27.p0), channel_id=1, source_target_pairs={{0,2},{1,3},{2,0},{3,1},{4,6},{5,7},{6,4},{7,5},{8,10},{9,11},{10,... | collective-permute-start | bytes 147464 | tf_op jit(solution)/shard_map/ppermute | solution.py:28
  24.5 1.5 %collective-permute-start.4 = (bf16[32,768]{1,0:T(8,128)(2,1)S(1)}, bf16[32,768]{1,0:T(8,128)(2,1)S(1)}, u32[]{:S(2)}, u32[]{:S(2)}) collective-permute-start(bf16[32,768]{1,0:T(8,128)(2,1)S(1)} %get-tuple-element.27.p0), channel_id=1, source_target_pairs={{0,3},{1,0},{2,1},{3,2},{4,7},{5,4},{6,5},{7,6},{8,11},{9,8},{10,9... | collective-permute-start | bytes 147464 | tf_op jit(solution)/shard_map/ppermute | solution.py:28
  26.1 2.1 %collective-permute-done.3.p2 = bf16[32,768]{1,0:T(8,128)(2,1)S(1)} collective-permute-done((bf16[32,768]{1,0:T(8,128)(2,1)S(1)}, bf16[32,768]{1,0:T(8,128)(2,1)S(1)}, u32[]{:S(2)}, u32[]{:S(2)}) %collective-permute-start.3) | collective-permute-done | bytes 49184 | tf_op jit(solution)/shard_map/ppermute | solution.py:28
  28.6 0.7 shard_map.143
  29.3 34.9 %all_to_all.15.kv_own = bf16[32,32,384]{2,1,0:T(8,128)(2,1)S(1)} all-to-all(bf16[32,32,384]{2,1,0:T(8,128)(2,1)S(1)} %get-tuple-element.30), channel_id=1, replica_groups=mesh['z'=8,'x'=4,'core'=2,'head'=4] {'z','x'}, dimensions={0} | all-to-all | bytes 1572864 | tf_op jit(solution)/shard_map/all_to_all | solution.py:42
  64.2 2.3 %collective-permute-done.5.kv_other = bf16[32,32,384]{2,1,0:T(8,128)(2,1)S(1)} collective-permute-done((bf16[32,32,384]{2,1,0:T(8,128)(2,1)S(1)}, bf16[32,32,384]{2,1,0:T(8,128)(2,1)S(1)}, u32[]{:S(2)}, u32[]{:S(2)}) %collective-permute-start.5) | collective-permute-done | bytes 786464 | tf_op jit(solution)/shard_map/ppermute | solution.py:28
  66.5 1.9 %shard_map.144.p0 = bf16[32,768]{1,0:T(8,128)(2,1)S(1)} custom-call(s32[4]{0:T(128)S(1)} %pad_add_fusion.where_ref, bf16[32,32,384]{2,1,0:T(8,128)(2,1)S(1)} %all_to_all.15.kv_own, bf16[32,32,384]{2,1,0:T(8,128)(2,1)S(1)} %collective-permute-done.5.kv_other, bf16[32,192]{1,0:T(8,128)(2,1)S(1)} %get-tuple-element.31.query, ...), custom_call_target="tpu_custom_call" | custom-call | flops 1073741824 | bytes 4194304 | tf_op jit(solution)/shard_map/pallas_call | solution.py:223
  68.4 0.7 collective-permute-start.6
  69.1 3.3 %collective-permute-start.7 = (bf16[32,768]{1,0:T(8,128)(2,1)S(1)}, bf16[32,768]{1,0:T(8,128)(2,1)S(1)}, u32[]{:S(2)}, u32[]{:S(2)}) collective-permute-start(bf16[32,768]{1,0:T(8,128)(2,1)S(1)} %shard_map.144.p0), channel_id=1, source_target_pairs={{0,2},{1,3},{2,0},{3,1},{4,6},{5,7},{6,4},{7,5},{8,10},{9,11},{10,... | collective-permute-start | bytes 147464 | tf_op jit(solution)/shard_map/ppermute | solution.py:28
  72.9 0.9 %collective-permute-done.6.p1 = bf16[32,768]{1,0:T(8,128)(2,1)S(1)} collective-permute-done((bf16[32,768]{1,0:T(8,128)(2,1)S(1)}, bf16[32,768]{1,0:T(8,128)(2,1)S(1)}, u32[]{:S(2)}, u32[]{:S(2)}) %collective-permute-start.6) | collective-permute-done | bytes 49184 | tf_op jit(solution)/shard_map/ppermute | solution.py:28
  73.8 1.5 %collective-permute-done.7.p2 = bf16[32,768]{1,0:T(8,128)(2,1)S(1)} collective-permute-done((bf16[32,768]{1,0:T(8,128)(2,1)S(1)}, bf16[32,768]{1,0:T(8,128)(2,1)S(1)}, u32[]{:S(2)}, u32[]{:S(2)}) %collective-permute-start.7) | collective-permute-done | bytes 49184 | tf_op jit(solution)/shard_map/ppermute | solution.py:28
  75.2 1.3 %collective-permute-done.8.p3 = bf16[32,768]{1,0:T(8,128)(2,1)S(1)} collective-permute-done((bf16[32,768]{1,0:T(8,128)(2,1)S(1)}, bf16[32,768]{1,0:T(8,128)(2,1)S(1)}, u32[]{:S(2)}, u32[]{:S(2)}) %collective-permute-start.8) | collective-permute-done | bytes 49184 | tf_op jit(solution)/shard_map/ppermute | solution.py:28
  76.5 1.3 %shard_map.145 = (f32[32,192]{1,0:T(8,128)S(1)}, bf16[4,32,192]{2,1,0:T(8,128)(2,1)S(1)}) custom-call(s32[4]{0:T(128)S(1)} %pad_add_fusion.where_ref, bf16[32,768]{1,0:T(8,128)(2,1)S(1)} %shard_map.144.p0, bf16[32,768]{1,0:T(8,128)(2,1)S(1)} %collective-permute-done.6.p1, bf16[32,768]{1,0:T(8,128)(2,1)S(1)} %collective-permute-done.7.p2, ...), custom_call_target="tpu_custom_call" | custom-call | flops 1073741824 | bytes 4194304 | tf_op jit(solution)/shard_map/pallas_call | solution.py:223
  77.8 8.2 %all_to_all.16 = bf16[4,32,192]{2,1,0:T(8,128)(2,1)S(1)} all-to-all(bf16[4,32,192]{2,1,0:T(8,128)(2,1)S(1)} %get-tuple-element.36), channel_id=1, replica_groups=mesh['z'=8,'x'=4,'core'=2,'head'=4] {'head'}, dimensions={0} | all-to-all | bytes 98304 | tf_op jit(solution)/shard_map/all_to_all | solution.py:42
  86.0 0.6 add_convert_fusion
  (36 shorter events, 1.1 us)
Async XLA Ops:
  0.6 0.9 %copy-start.3 = (bf16[768,128]{1,0:T(8,128)(2,1)S(1)}, bf16[768,128]{1,0:T(8,128)(2,1)}, u32[]{:S(2)}) copy-start(bf16[768,128]{1,0:T(8,128)(2,1)} %atoms.3) | copy-start | bytes 589828
  1.6 0.7 copy-start.8
  2.8 9.3 %collective-permute-start.1 = (bf16[80,128]{1,0:T(8,128)(2,1)S(1)}, bf16[80,128]{1,0:T(8,128)(2,1)S(1)}, u32[]{:S(2)}, u32[]{:S(2)}) collective-permute-start(bf16[80,128]{1,0:T(8,128)(2,1)S(1)} %get-tuple-element.24), channel_id=1, source_target_pairs={{4,0},{8,4},{12,8},{16,12},{20,16},{24,20},{28,24},{32,28},{36,32}... | collective-permute-start | bytes 61448 | tf_op jit(solution)/shard_map/ppermute | solution.py:34
  5.0 7.1 %collective-permute-start = (bf16[48,128]{1,0:T(8,128)(2,1)S(1)}, bf16[48,128]{1,0:T(8,128)(2,1)S(1)}, u32[]{:S(2)}, u32[]{:S(2)}) collective-permute-start(bf16[48,128]{1,0:T(8,128)(2,1)S(1)} %get-tuple-element.23), channel_id=1, source_target_pairs={{0,4},{4,8},{8,12},{12,16},{16,20},{20,24},{24,28},{28,32},{32,36}... | collective-permute-start | bytes 36872 | tf_op jit(solution)/shard_map/ppermute | solution.py:34
  7.1 9.5 %copy-start.4 = (bf16[768,128]{1,0:T(8,128)(2,1)S(1)}, bf16[768,128]{1,0:T(8,128)(2,1)}, u32[]{:S(2)}) copy-start(bf16[768,128]{1,0:T(8,128)(2,1)} %atoms.3) | copy-start | bytes 589828
  7.1 9.5 %copy-start.5 = (bf16[32,768]{1,0:T(8,128)(2,1)S(1)}, bf16[32,768]{1,0:T(8,128)(2,1)}, u32[]{:S(2)}) copy-start(bf16[32,768]{1,0:T(8,128)(2,1)} %w_token.1) | copy-start | bytes 147460
  7.2 9.5 %copy-start.7 = (bf16[128,3,32]{0,2,1:T(8,128)(2,1)S(1)}, bf16[128,3,32]{0,2,1:T(8,128)(2,1)}, u32[]{:S(2)}) copy-start(bf16[128,3,32]{0,2,1:T(8,128)(2,1)} %param.17) | copy-start | bytes 73732
  7.2 9.5 %copy-start.9 = (s32[32]{0:T(128)S(1)}, s32[32]{0:T(128)}, u32[]{:S(2)}) copy-start(s32[32]{0:T(128)} %count_ref.3) | copy-start | bytes 388
  12.1 17.2 %all-to-all-start = ((bf16[16,32,512]{2,1,0:T(8,128)(2,1)}), bf16[16,32,512]{2,1,0:T(8,128)(2,1)S(1)}, u32[]{:S(2)}, u32[]{:S(2)}) async-start(bf16[16,32,512]{2,1,0:T(8,128)(2,1)} %shard_map.141), calls=%async_computation | async-start | bytes 1048576 | tf_op jit(solution)/shard_map/all_to_all | solution.py:42
  16.7 9.3 %copy-start.11 = (bf16[768]{0:T(1024)(128)(2,1)S(1)}, bf16[768]{0:T(1024)(128)(2,1)}, u32[]{:S(2)}) copy-start(bf16[768]{0:T(1024)(128)(2,1)} %param.19) | copy-start | bytes 4612
  16.7 11.9 %copy-start = (bf16[768,4,192]{0,2,1:T(8,128)(2,1)S(1)}, bf16[768,4,192]{0,2,1:T(8,128)(2,1)}, u32[]{:S(2)}) copy-start(bf16[768,4,192]{0,2,1:T(8,128)(2,1)} %param.20) | copy-start | bytes 3538948
  16.7 11.9 %copy-start.6 = (bf16[32,768]{1,0:T(8,128)(2,1)S(1)}, bf16[32,768]{1,0:T(8,128)(2,1)}, u32[]{:S(2)}) copy-start(bf16[32,768]{1,0:T(8,128)(2,1)} %single.1) | copy-start | bytes 147460
  19.8 6.3 %collective-permute-start.2 = (bf16[32,768]{1,0:T(8,128)(2,1)S(1)}, bf16[32,768]{1,0:T(8,128)(2,1)S(1)}, u32[]{:S(2)}, u32[]{:S(2)}) collective-permute-start(bf16[32,768]{1,0:T(8,128)(2,1)S(1)} %get-tuple-element.27.p0), channel_id=1, source_target_pairs={{0,1},{1,2},{2,3},{3,0},{4,5},{5,6},{6,7},{7,4},{8,9},{9,10},{10,1... | collective-permute-start | bytes 147464 | tf_op jit(solution)/shard_map/ppermute | solution.py:28
  21.8 6.4 %collective-permute-start.3 = (bf16[32,768]{1,0:T(8,128)(2,1)S(1)}, bf16[32,768]{1,0:T(8,128)(2,1)S(1)}, u32[]{:S(2)}, u32[]{:S(2)}) collective-permute-start(bf16[32,768]{1,0:T(8,128)(2,1)S(1)} %get-tuple-element.27.p0), channel_id=1, source_target_pairs={{0,2},{1,3},{2,0},{3,1},{4,6},{5,7},{6,4},{7,5},{8,10},{9,11},{10,... | collective-permute-start | bytes 147464 | tf_op jit(solution)/shard_map/ppermute | solution.py:28
  24.5 4.1 %collective-permute-start.4 = (bf16[32,768]{1,0:T(8,128)(2,1)S(1)}, bf16[32,768]{1,0:T(8,128)(2,1)S(1)}, u32[]{:S(2)}, u32[]{:S(2)}) collective-permute-start(bf16[32,768]{1,0:T(8,128)(2,1)S(1)} %get-tuple-element.27.p0), channel_id=1, source_target_pairs={{0,3},{1,0},{2,1},{3,2},{4,7},{5,4},{6,5},{7,6},{8,11},{9,8},{10,9... | collective-permute-start | bytes 147464 | tf_op jit(solution)/shard_map/ppermute | solution.py:28
  29.3 37.2 %copy-start.2 = (bf16[192,768]{1,0:T(8,128)(2,1)S(1)}, bf16[192,768]{1,0:T(8,128)(2,1)}, u32[]{:S(2)}) copy-start(bf16[192,768]{1,0:T(8,128)(2,1)} %w_out.1) | copy-start | bytes 884740
  64.2 2.3 %collective-permute-start.5 = (bf16[32,32,384]{2,1,0:T(8,128)(2,1)S(1)}, bf16[32,32,384]{2,1,0:T(8,128)(2,1)S(1)}, u32[]{:S(2)}, u32[]{:S(2)}) collective-permute-start(bf16[32,32,384]{2,1,0:T(8,128)(2,1)S(1)} %all_to_all.15.kv_own), channel_id=1, source_target_pairs={{0,4},{4,0},{1,5},{5,1},{2,6},{6,2},{3,7},{7,3},{8,12},{12,8},{9,1... | collective-permute-start | bytes 2359304 | tf_op jit(solution)/shard_map/ppermute | solution.py:28
  66.5 6.2 %copy-start.10 = (bf16[768,2,384]{2,1,0:T(2,128)(2,1)S(1)}, bf16[768,2,384]{2,1,0:T(2,128)(2,1)}, u32[]{:S(2)}) copy-start(bf16[768,2,384]{2,1,0:T(2,128)(2,1)} %param.24) | copy-start | bytes 3538948
  68.4 4.5 %copy-start.12 = (bf16[768]{0:T(1024)(128)(2,1)S(1)}, bf16[768]{0:T(1024)(128)(2,1)}, u32[]{:S(2)}) copy-start(bf16[768]{0:T(1024)(128)(2,1)} %param.23) | copy-start | bytes 4612
  68.4 8.2 %copy-start.1 = (bf16[384,768]{1,0:T(8,128)(2,1)S(1)}, bf16[384,768]{1,0:T(8,128)(2,1)}, u32[]{:S(2)}) copy-start(bf16[384,768]{1,0:T(8,128)(2,1)} %w_down.1) | copy-start | bytes 1769476
  68.4 5.4 %collective-permute-start.6 = (bf16[32,768]{1,0:T(8,128)(2,1)S(1)}, bf16[32,768]{1,0:T(8,128)(2,1)S(1)}, u32[]{:S(2)}, u32[]{:S(2)}) collective-permute-start(bf16[32,768]{1,0:T(8,128)(2,1)S(1)} %shard_map.144.p0), channel_id=1, source_target_pairs={{0,1},{1,2},{2,3},{3,0},{4,5},{5,6},{6,7},{7,4},{8,9},{9,10},{10,1... | collective-permute-start | bytes 147464 | tf_op jit(solution)/shard_map/ppermute | solution.py:28
  69.1 6.2 %collective-permute-start.7 = (bf16[32,768]{1,0:T(8,128)(2,1)S(1)}, bf16[32,768]{1,0:T(8,128)(2,1)S(1)}, u32[]{:S(2)}, u32[]{:S(2)}) collective-permute-start(bf16[32,768]{1,0:T(8,128)(2,1)S(1)} %shard_map.144.p0), channel_id=1, source_target_pairs={{0,2},{1,3},{2,0},{3,1},{4,6},{5,7},{6,4},{7,5},{8,10},{9,11},{10,... | collective-permute-start | bytes 147464 | tf_op jit(solution)/shard_map/ppermute | solution.py:28
  72.4 4.1 %collective-permute-start.8 = (bf16[32,768]{1,0:T(8,128)(2,1)S(1)}, bf16[32,768]{1,0:T(8,128)(2,1)S(1)}, u32[]{:S(2)}, u32[]{:S(2)}) collective-permute-start(bf16[32,768]{1,0:T(8,128)(2,1)S(1)} %shard_map.144.p0), channel_id=1, source_target_pairs={{0,3},{1,0},{2,1},{3,2},{4,7},{5,4},{6,5},{7,6},{8,11},{9,8},{10,9... | collective-permute-start | bytes 147464 | tf_op jit(solution)/shard_map/ppermute | solution.py:28

commit v2 on v1

--- a/solution.py
+++ b/solution.py
@@ -28,10 +28,9 @@
     return lax.ppermute(block, axis, [(i, (i + distance) % size) for i in range(size)])
 
 
-def from_behind(block, axis, distance):
-    devices = range(lax.axis_size(axis))
-    route = [(i - distance, i) for i in devices if i - distance in devices]
-    return lax.ppermute(block, axis, route)
+def swapped(block, axis, first):
+    low = range(first, lax.axis_size(axis) - 1, 2)
+    return lax.ppermute(block, axis, [(i, i + 1) for i in low] + [(i + 1, i) for i in low])
 
 
 def of_everyone(partial):
@@ -56,30 +55,42 @@
     return centred * lax.rsqrt(spread + norm_eps) * gain
 
 
-def halo_kernel(count_ref, atoms, head_rows, tail_rows, rows):
-    live = live_atoms(count_ref)
-    rows[...] = atoms[...].astype(f32)
-    head_rows[...] = atoms[0:HEADROWS]
-    tail_rows[...] = rows[pl.ds(live - TAIL, TAIL), :].astype(bf16)
-
-
-def pair_kernel(pair, w_bias, out):
-    half = pair.shape[1] // 2
-    w = w_bias[...].astype(f32)
-    blank = jnp.zeros_like(w)
-    both = jnp.concatenate(
-        [jnp.concatenate([w, blank], axis=1), jnp.concatenate([blank, w], axis=1)], axis=0
-    ).astype(bf16)
-    terms = []
-    for q in range(pair.shape[0]):
-        keys = jnp.concatenate([pair[q, :half], pair[q, half:]], axis=1)
-        term = lax.dot_general(both, keys, NT, preferred_element_type=f32)
-        terms.append(jnp.concatenate([term[:H], term[H:]], axis=1))
-    out[...] = jnp.stack(terms, axis=1).astype(bf16)
+def halo_kernel(where_ref, count_hbm, atoms_hbm, across, within, counts, atoms, rows, sems):
+    copies = [
+        pltpu.make_async_copy(count_hbm, counts, sems.at[0]),
+        pltpu.make_async_copy(atoms_hbm, atoms, sems.at[1]),
+    ]
+    for copy in copies:
+        copy.start()
+    for copy in copies:
+        copy.wait()
+    live = live_atoms(counts)
+    rows[0 : atoms.shape[0]] = atoms[...].astype(f32)
+    head_rows = rows[0:HEADROWS]
+    tail_rows = rows[pl.ds(live - TAIL, HEADROWS), :]
+    even = where_ref[2] == 0
+    across[...] = jnp.where(even, head_rows, tail_rows).astype(bf16)
+    within[...] = jnp.where(even, tail_rows, head_rows).astype(bf16)
+
+
+def pair_kernel(pair, w_bias, after, out):
+    tokens, keys, channels = pair.shape
+    heads = w_bias.shape[0]
+    count = 8
+    rows = jnp.broadcast_to(w_bias[...].astype(f32)[:, None, :], (heads, count, channels))
+    rows = rows.reshape(heads * count, channels)
+    query = lax.broadcasted_iota(jnp.int32, rows.shape, 0) % count
+    spread = jnp.concatenate(
+        [jnp.where(query == q, rows, 0.0).astype(bf16) for q in range(count)], axis=1
+    )
+    for at in range(0, tokens, count):
+        keyed = jnp.concatenate([pair[at + q] for q in range(count)], axis=1)
+        terms = lax.dot_general(spread, keyed, NT, preferred_element_type=f32)
+        out[:, at : at + count, :] = terms.reshape(heads, count, keys).astype(bf16)
 
 
 def atom_kernel(
-    where_ref, count_ref, counts_row, atoms, previous, following, w_atom, w_token, partial, mix, rows
+    where_ref, count_ref, counts_row, atoms, across, within, w_atom, w_token, partial, mix, rows
 ):
     slots = atoms.shape[0]
     tokens = counts_row.shape[1]
@@ -87,19 +98,22 @@
     live = live_atoms(count_ref)
     first = where_ref[0] == 0
     last = where_ref[0] == where_ref[1]
-    rows[0:TAIL] = previous[...].astype(f32)
+    even = where_ref[2] == 0
+    far, near = across[...].astype(f32), within[...].astype(f32)
+    rows[0:TAIL] = jnp.where(even, far, near)[:TAIL]
     rows[TAIL : TAIL + slots] = atoms[...].astype(f32)
     rows[TAIL + slots :] = jnp.zeros((HEADROWS, atoms.shape[1]), f32)
-    rows[pl.ds(TAIL + live, HEADROWS), :] = following[...].astype(f32)
+    rows[pl.ds(TAIL + live, HEADROWS), :] = jnp.where(even, near, far)
     keyed = rows[...].astype(bf16)
 
-    def projected(part):
-        w = w_atom[part * width : (part + 1) * width, :]
-        return lax.dot_general(keyed, w, NT, preferred_element_type=f32)
-
-    queries = projected(0)[TAIL : TAIL + slots].astype(bf16)
-    keys = projected(1).astype(bf16)
-    values = projected(2).astype(bf16)
+    def weight(part):
+        return w_atom[part * width : (part + 1) * width, :]
+
+    queries = lax.dot_general(keyed[TAIL : TAIL + slots], weight(0), NT, preferred_element_type=f32)
+    queries = queries.astype(bf16)
+    keys = lax.dot_general(keyed, weight(1), NT, preferred_element_type=f32).astype(bf16)
+    values = lax.dot_general(weight(2), keyed, NT, preferred_element_type=f32)
+    values = jnp.concatenate([values, jnp.ones((16, values.shape[1]), f32)], axis=0).astype(bf16)
 
     counts = jnp.broadcast_to(counts_row[...].astype(f32), (tokens, tokens))
     token_row = lax.broadcasted_iota(jnp.int32, (tokens, tokens), 0)
@@ -110,27 +124,30 @@
     row = lax.broadcasted_iota(jnp.int32, (QBLOCK, KBLOCK), 0)
     lane = lax.broadcasted_iota(jnp.int32, (QBLOCK, KBLOCK), 1)
     offset = lane - (row // QWIN) * QWIN
-    in_window = (offset >= 0) & (offset < KWIN)
+    in_window = jnp.where((offset >= 0) & (offset < KWIN), 0.0, masked_value)
+    key_lane = lax.broadcasted_iota(jnp.int32, (1, KBLOCK), 1)
     low = jnp.where(first, 0, -slots)
     high = jnp.where(last, live, 4 * slots)
-    out_row = lax.broadcasted_iota(jnp.int32, (QBLOCK, width), 0)
+    query_lane = lax.broadcasted_iota(jnp.int32, (width, QBLOCK), 1)
     slot = lax.broadcasted_iota(jnp.int32, (tokens, QBLOCK), 1).astype(f32)
     totals = jnp.zeros((tokens, width), f32)
     for b in range(slots // QBLOCK):
         at = b * QBLOCK
+        key_pos = key_lane + (at - TAIL)
+        in_sequence = jnp.where((key_pos >= low) & (key_pos < high), 0.0, masked_value)
         scores = lax.dot_general(
             queries[at : at + QBLOCK], keys[at : at + KBLOCK], NT, preferred_element_type=f32
-        ) * width ** (-0.5)
-        key_pos = lane + (at - TAIL)
-        scores = jnp.where(in_window & (key_pos >= low) & (key_pos < high), scores, masked_value)
-        lifted = jnp.exp(scores - jnp.max(scores, axis=1, keepdims=True))
-        weights = (lifted / jnp.sum(lifted, axis=1, keepdims=True)).astype(bf16)
-        out = jnp.dot(weights, values[at : at + KBLOCK], preferred_element_type=f32)
-        out = jnp.where(out_row + at < live, out, 0.0)
-        mix[:, at : at + QBLOCK] = out.T.astype(bf16)
-        member = (slot + at >= starts) & (slot + at < starts + own)
-        totals = totals + jnp.dot(
-            jnp.where(member, 1.0, 0.0).astype(bf16), out.astype(bf16), preferred_element_type=f32
+        ) * width ** (-0.5) + (in_window + in_sequence)
+        lifted = jnp.exp(scores - jnp.max(scores, axis=1, keepdims=True)).astype(bf16)
+        summed = lax.dot_general(
+            values[:, at : at + KBLOCK], lifted, NT, preferred_element_type=f32
+        )
+        out = jnp.where(query_lane + at < live, summed[:width] / summed[width : width + 1], 0.0)
+        out = out.astype(bf16)
+        mix[:, at : at + QBLOCK] = out
+        member = jnp.where((slot + at >= starts) & (slot + at < starts + own), 1.0, 0.0)
+        totals = totals + lax.dot_general(
+            member.astype(bf16), out, NT, preferred_element_type=f32
         )
     token_atoms = (totals / own).astype(bf16)
     partial[...] = jnp.dot(token_atoms, w_token[...], preferred_element_type=f32).astype(bf16)
@@ -150,11 +167,18 @@
         kv[i] = pair
 
 
-def attention_kernel(where_ref, kv_own, kv_other, query, gate, bias, w_out, partial, kv, scores):
+def attention_kernel(
+    where_ref, own0, own1, own2, own3, other0, other1, other2, other3, query, gate, bias, w_out,
+    partial, kv, scores
+):
     core = where_ref[2]
-    groups, tokens, width = kv_own.shape
-    kv[:, pl.ds(core, 1)] = kv_own[...].reshape(groups, 1, tokens, width)
-    kv[:, pl.ds(1 - core, 1)] = kv_other[...].reshape(groups, 1, tokens, width)
+    groups, tokens, width = own0.shape
+    for distance, (own, other) in enumerate(
+        ((own0, other0), (own1, other1), (own2, other2), (own3, other3))
+    ):
+        x = (where_ref[4] + 4 - distance) % 4
+        kv[:, pl.ds(x, 1), pl.ds(core, 1)] = own[...].reshape(groups, 1, 1, tokens, width)
+        kv[:, pl.ds(x, 1), pl.ds(1 - core, 1)] = other[...].reshape(groups, 1, 1, tokens, width)
     part = query.shape[1]
     size = part // 4
     rows = 4 * tokens
@@ -166,7 +190,7 @@
     lane = lax.broadcasted_iota(jnp.int32, (rows, reach), 1) - (reach - part)
     queries = jnp.where((lane >= head * size) & (lane < (head + 1) * size), spread, 0.0)
     queries = queries.astype(bf16)
-    keyed = kv[...].reshape(groups * 2 * tokens, width)
+    keyed = kv[...].reshape(groups * 8 * tokens, width)
     block = bias.shape[2]
     scale = size ** (-0.5)
     top = None
@@ -226,7 +250,7 @@
         in_specs=[scalar] * smem + [vmem] * (len(operands) - smem),
         out_specs=jax.tree.map(lambda _: vmem, out_shape),
         scratch_shapes=scratch,
-        compiler_params=pltpu.CompilerParams(vmem_limit_bytes=40 << 20),
+        compiler_params=pltpu.CompilerParams(vmem_limit_bytes=16 << 20),
         cost_estimate=pl.CostEstimate(flops=1 << 30, bytes_accessed=4 << 20, transcendentals=0),
     )(*operands)
 
@@ -254,35 +278,42 @@
             jnp.int32(lax.axis_size(TOK) - 1),
             lax.axis_index("core"),
             lax.axis_index("head"),
+            lax.axis_index("x"),
         ]
     ).astype(jnp.int32)
-    head_rows, tail_rows = call(
+    send = jax.ShapeDtypeStruct((HEADROWS, channels), bf16)
+    vmem = pl.BlockSpec(memory_space=pltpu.VMEM)
+    hbm = pl.BlockSpec(memory_space=pl.ANY)
+    sent_across, sent_within = pl.pallas_call(
         halo_kernel,
-        (
-            jax.ShapeDtypeStruct((HEADROWS, channels), bf16),
-            jax.ShapeDtypeStruct((TAIL, channels), bf16),
-        ),
-        (atom_counts, atoms),
-        [pltpu.VMEM((slots, channels), f32)],
-        1,
-    )
-    pair, head_rows, tail_rows = lax.optimization_barrier((pair, head_rows, tail_rows))
-    following = from_behind(head_rows, TOK, -1)
-    previous = from_behind(tail_rows, TOK, 1)
-
+        out_shape=(send, send),
+        in_specs=[pl.BlockSpec(memory_space=pltpu.SMEM), hbm, hbm],
+        out_specs=(vmem, vmem),
+        scratch_shapes=[
+            pltpu.SMEM((tokens,), jnp.int32),
+            pltpu.VMEM((slots, channels), bf16),
+            pltpu.VMEM((slots + HEADROWS, channels), f32),
+            pltpu.SemaphoreType.DMA((2,)),
+        ],
+        compiler_params=pltpu.CompilerParams(vmem_limit_bytes=4 << 20),
+        cost_estimate=pl.CostEstimate(flops=1 << 33, bytes_accessed=32 << 20, transcendentals=0),
+    )(
+        where_at,
+        pltpu.with_memory_space_constraint(atom_counts, pltpu.HBM),
+        pltpu.with_memory_space_constraint(atoms, pltpu.HBM),
+    )
+    across = swapped(sent_across, TOK, 1)
+    within = swapped(sent_within, TOK, 0)
     keys = pair.shape[1]
     pair_term = pl.pallas_call(
         pair_kernel,
         out_shape=jax.ShapeDtypeStruct((H, tokens, keys), bf16),
-        grid=(4,),
-        in_specs=[
-            pl.BlockSpec((tokens // 4, keys, pair.shape[2]), lambda i: (i, 0, 0)),
-            pl.BlockSpec((H, pair.shape[2]), lambda i: (0, 0)),
-        ],
-        out_specs=pl.BlockSpec((H, tokens // 4, keys), lambda i: (0, i, 0)),
+        in_specs=[vmem, vmem, hbm],
+        out_specs=vmem,
+        compiler_params=pltpu.CompilerParams(vmem_limit_bytes=16 << 20),
         cost_estimate=pl.CostEstimate(flops=2 << 30, bytes_accessed=8 << 20, transcendentals=0),
-    )(pair, w_pair_bias.T)
-    pair_term, previous, following = lax.optimization_barrier((pair_term, previous, following))
+    )(pair, w_pair_bias.T, sent_across)
+    pair_term, across, within = lax.optimization_barrier((pair_term, across, within))
     bias = exchanged(pair_term, "head")
 
     width = w_atom.shape[2]
@@ -297,8 +328,8 @@
             atom_counts,
             atom_counts.reshape(1, tokens),
             atoms,
-            previous,
-            following,
+            across,
+            within,
             w_atom.transpose(1, 2, 0).reshape(3 * width, channels),
             w_atom_token,
         ),
@@ -310,7 +341,7 @@
         projection_kernel,
         (
             jax.ShapeDtypeStruct((tokens, model), f32),
-            jax.ShapeDtypeStruct((32, tokens, 2 * quarter), bf16),
+            jax.ShapeDtypeStruct((8, tokens, 2 * quarter), bf16),
             jax.ShapeDtypeStruct((tokens, quarter), bf16),
             jax.ShapeDtypeStruct((tokens, quarter), f32),
         ),
@@ -324,14 +355,15 @@
         0,
     )
     kv, bias = lax.optimization_barrier((kv, bias))
-    kv_own = exchanged(kv, ("z", "x"))
-    kv_other = sent_around(kv_own, "core", 1)
+    kv_own = exchanged(kv, "z")
+    kv_own = [kv_own] + [sent_around(kv_own, "x", d) for d in (1, 2, 3)]
+    kv_other = [sent_around(piece, "core", 1) for piece in kv_own]
     partial = call(
         attention_kernel,
         jax.ShapeDtypeStruct((tokens, model), bf16),
-        (where_at, kv_own, kv_other, query, gate, bias, w_out),
+        (where_at, *kv_own, *kv_other, query, gate, bias, w_out),
         [
-            pltpu.VMEM((32, 2, tokens, 2 * quarter), bf16),
+            pltpu.VMEM((8, 4, 2, tokens, 2 * quarter), bf16),
             pltpu.VMEM((4, 4 * tokens, bias.shape[2]), f32),
         ],
         1,

time: 87.1 us -> 77.6 us (0.89)
  blocking collectives: 43.1 us -> 27.7 us
  waiting for transfers between devices: 8.53 us -> 15 us
  starting transfers between devices: 19.3 us -> 22.4 us
  Pallas kernels: 12.4 us -> 10.6 us
  local copies, waits for them, and re-layouts: 1.8 us -> 0.32 us
    all_to_all x2, blocking collectives: 43.1 us -> 27.7 us  [exchanged(): return lax.all_to_all(pieces, axis, split_axis=0, concat_axis=0, tiled=True)]
    ppermute x7 -> x13, waiting for transfers between devices: 8.52 us -> 15 us  [sent_around(): lax.ppermute(block, axis, [(i, (i + distance) % size) for i in range(size)])]
    ppermute x7 -> x13, starting transfers between devices: 10.5 us -> 13.9 us  [sent_around(): lax.ppermute(block, axis, [(i, (i + distance) % size) for i in range(size)])]
    pallas_call x1, Pallas kernels: 4.91 us -> 2.28 us  [shards(): pl.pallas_call(pair_kernel, out_shape=jax.ShapeDtypeStruct((H, tokens, ke...]
    pallas_call x0 -> x1, Pallas kernels: none -> 1.78 us  [shards(): pl.pallas_call(halo_kernel, out_shape=(send, send), in_specs=[pl.BlockSpe...]
    unnamed x27, local copies, waits for them, and re-layouts: 1.79 us -> 0.22 us
    pallas_call x5 -> x4, Pallas kernels: 7.48 us -> 6.53 us  [call(): pl.pallas_call(kernel, out_shape=out_shape, in_specs=[scalar] * smem + [v...]
  transfers between devices with their start and end apart: 10 -> 16, of which waited for: 7 -> 9; matrix products, arithmetic and copies ran while one was open for 0% -> 0% of each run, Pallas kernels for 10% -> 7%
where the time goes in v2:
time: 77.6 us; the launch traced here: 77.4 us
  blocking collectives  27.7 us (36%)
  starting transfers between devices  22.4 us (29%)
  waiting for transfers between devices  15 us (19%)
  Pallas kernels  10.6 us (14%)
  between operations  0.8 us (1%)
    all_to_all x2, blocking collectives, exchanged(): return lax.all_to_all(pieces, axis, split_axis=0, concat_axis=0, tiled=True)  27.7 us
    ppermute x13, waiting for transfers between devices, sent_around(): lax.ppermute(block, axis, [(i, (i + distance) % size) for i in range(size)])  15 us
    ppermute x13, starting transfers between devices, sent_around(): lax.ppermute(block, axis, [(i, (i + distance) % size) for i in range(size)])  13.9 us
    pallas_call x4, Pallas kernels, call(): pl.pallas_call(kernel, out_shape=out_shape, in_specs=[scalar] * smem + [v...  6.53 us
    all_to_all x1, starting transfers between devices, exchanged(): return lax.all_to_all(pieces, axis, split_axis=0, concat_axis=0, tiled=True)  4.48 us
    ppermute x2, starting transfers between devices, swapped(): lax.ppermute(block, axis, [(i, i + 1) for i in low] + [(i + 1, i) for i i...  3.94 us
    pallas_call x1, Pallas kernels, shards(): pl.pallas_call(pair_kernel, out_shape=jax.ShapeDtypeStruct((H, tokens, ke...  2.28 us
    pallas_call x1, Pallas kernels, shards(): pl.pallas_call(halo_kernel, out_shape=(send, send), in_specs=[pl.BlockSpe...  1.78 us
  transfers between devices with their start and end apart: 16, of which 9 were waited for; matrix products, arithmetic and copies ran while one was open for 0% of the time, Pallas kernels for 7%

profile of v2, /device:TPU:6, one launch (start us, length us, event | category | flops | bytes accessed | tf_op | source)
XLA Modules:
  0.0 77.4 jit_solution(15788872104969936778)
XLA Ops:
  0.7 1.8 %shard_map.140 = (bf16[80,128]{1,0:T(8,128)(2,1)S(1)}, bf16[80,128]{1,0:T(8,128)(2,1)S(1)}) custom-call(s32[5]{0:T(128)S(1)} %stack.19.where_ref, s32[32]{0:T(128)} %count_ref.1, bf16[768,128]{1,0:T(8,128)(2,1)} %atoms.1), custom_call_target="tpu_custom_call" | custom-call | flops 8589934592 | bytes 33554432 | tf_op jit(solution)/shard_map/pallas_call | solution.py:287
  2.5 2.2 %collective-permute-start = (bf16[80,128]{1,0:T(8,128)(2,1)S(1)}, bf16[80,128]{1,0:T(8,128)(2,1)S(1)}, u32[]{:S(2)}, u32[]{:S(2)}) collective-permute-start(bf16[80,128]{1,0:T(8,128)(2,1)S(1)} %get-tuple-element.17.after), channel_id=1, source_target_pairs={{4,8},{12,16},{20,24},{28,32},{36,40},{44,48},{52,56},{60,64},{68,... | collective-permute-start | bytes 61448 | tf_op jit(solution)/shard_map/ppermute | solution.py:33
  4.7 1.8 %collective-permute-start.1 = (bf16[80,128]{1,0:T(8,128)(2,1)S(1)}, bf16[80,128]{1,0:T(8,128)(2,1)S(1)}, u32[]{:S(2)}, u32[]{:S(2)}) collective-permute-start(bf16[80,128]{1,0:T(8,128)(2,1)S(1)} %get-tuple-element.18), channel_id=1, source_target_pairs={{0,4},{8,12},{16,20},{24,28},{32,36},{40,44},{48,52},{56,60},{64,6... | collective-permute-start | bytes 61448 | tf_op jit(solution)/shard_map/ppermute | solution.py:33
  6.5 2.3 %shard_map.141 = bf16[16,32,512]{2,1,0:T(8,128)(2,1)} custom-call(bf16[32,512,128]{2,1,0:T(8,128)(2,1)S(1)} %copy-done, bf16[16,128]{1,0:T(8,128)(2,1)S(1)} %bitcast.18, bf16[80,128]{1,0:T(8,128)(2,1)S(1)} %get-tuple-element.17.after), custom_call_target="tpu_custom_call" | custom-call | flops 2147483648 | bytes 8388608 | tf_op jit(solution)/shard_map/pallas_call | solution.py:308
  8.8 4.5 %all-to-all-start = ((bf16[16,32,512]{2,1,0:T(8,128)(2,1)}), bf16[16,32,512]{2,1,0:T(8,128)(2,1)S(1)}, u32[]{:S(2)}, u32[]{:S(2)}) async-start(bf16[16,32,512]{2,1,0:T(8,128)(2,1)} %shard_map.141), calls=%async_computation | async-start | bytes 1048576 | tf_op jit(solution)/shard_map/all_to_all | solution.py:41
  13.3 2.7 %shard_map.142 = (bf16[32,768]{1,0:T(8,128)(2,1)S(1)}, bf16[32,768]{1,0:T(8,128)(2,1)}) custom-call(s32[5]{0:T(128)S(1)} %stack.19.where_ref, s32[32]{0:T(128)S(1)} %copy-done.9, s32[1,32]{1,0:T(1,128)S(1)} %bitcast.19, bf16[768,128]{1,0:T(8,128)(2,1)S(1)} %copy-done.4, bf16[80,128]{1,0:T(8,128)(2,1)S(1)} %collective-permute-done.across, ...), custom_call_target="tpu_custom_call" | custom-call | flops 1073741824 | bytes 4194304 | tf_op jit(solution)/shard_map/pallas_call | solution.py:247
  16.0 2.0 %collective-permute-start.2 = (bf16[32,768]{1,0:T(8,128)(2,1)S(1)}, bf16[32,768]{1,0:T(8,128)(2,1)S(1)}, u32[]{:S(2)}, u32[]{:S(2)}) collective-permute-start(bf16[32,768]{1,0:T(8,128)(2,1)S(1)} %get-tuple-element.21.p0), channel_id=1, source_target_pairs={{0,1},{1,2},{2,3},{3,0},{4,5},{5,6},{6,7},{7,4},{8,9},{9,10},{10,1... | collective-permute-start | bytes 147464 | tf_op jit(solution)/shard_map/ppermute | solution.py:28
  18.0 2.7 %collective-permute-start.3 = (bf16[32,768]{1,0:T(8,128)(2,1)S(1)}, bf16[32,768]{1,0:T(8,128)(2,1)S(1)}, u32[]{:S(2)}, u32[]{:S(2)}) collective-permute-start(bf16[32,768]{1,0:T(8,128)(2,1)S(1)} %get-tuple-element.21.p0), channel_id=1, source_target_pairs={{0,2},{1,3},{2,0},{3,1},{4,6},{5,7},{6,4},{7,5},{8,10},{9,11},{10,... | collective-permute-start | bytes 147464 | tf_op jit(solution)/shard_map/ppermute | solution.py:28
  20.7 1.5 %collective-permute-start.4 = (bf16[32,768]{1,0:T(8,128)(2,1)S(1)}, bf16[32,768]{1,0:T(8,128)(2,1)S(1)}, u32[]{:S(2)}, u32[]{:S(2)}) collective-permute-start(bf16[32,768]{1,0:T(8,128)(2,1)S(1)} %get-tuple-element.21.p0), channel_id=1, source_target_pairs={{0,3},{1,0},{2,1},{3,2},{4,7},{5,4},{6,5},{7,6},{8,11},{9,8},{10,9... | collective-permute-start | bytes 147464 | tf_op jit(solution)/shard_map/ppermute | solution.py:28
  22.2 2.3 %collective-permute-done.2.p1 = bf16[32,768]{1,0:T(8,128)(2,1)S(1)} collective-permute-done((bf16[32,768]{1,0:T(8,128)(2,1)S(1)}, bf16[32,768]{1,0:T(8,128)(2,1)S(1)}, u32[]{:S(2)}, u32[]{:S(2)}) %collective-permute-start.2) | collective-permute-done | bytes 49184 | tf_op jit(solution)/shard_map/ppermute | solution.py:28
  24.5 1.3 %collective-permute-done.3.p2 = bf16[32,768]{1,0:T(8,128)(2,1)S(1)} collective-permute-done((bf16[32,768]{1,0:T(8,128)(2,1)S(1)}, bf16[32,768]{1,0:T(8,128)(2,1)S(1)}, u32[]{:S(2)}, u32[]{:S(2)}) %collective-permute-start.3) | collective-permute-done | bytes 49184 | tf_op jit(solution)/shard_map/ppermute | solution.py:28
  26.6 18.3 %all_to_all.15.own0 = bf16[8,32,384]{2,1,0:T(8,128)(2,1)S(1)} all-to-all(bf16[8,32,384]{2,1,0:T(8,128)(2,1)S(1)} %get-tuple-element.24), channel_id=1, replica_groups=mesh['z'=8,'x'=4,'core'=2,'head'=4] {'z'}, dimensions={0} | all-to-all | bytes 393216 | tf_op jit(solution)/shard_map/all_to_all | solution.py:41
  44.9 2.1 %collective-permute-start.7 = (bf16[8,32,384]{2,1,0:T(8,128)(2,1)S(1)}, bf16[8,32,384]{2,1,0:T(8,128)(2,1)S(1)}, u32[]{:S(2)}, u32[]{:S(2)}) collective-permute-start(bf16[8,32,384]{2,1,0:T(8,128)(2,1)S(1)} %all_to_all.15.own0), channel_id=1, source_target_pairs={{0,24},{8,0},{16,8},{24,16},{1,25},{9,1},{17,9},{25,17},{2,26},{10... | collective-permute-start | bytes 589832 | tf_op jit(solution)/shard_map/ppermute | solution.py:28
  47.0 1.1 %collective-permute-start.5 = (bf16[8,32,384]{2,1,0:T(8,128)(2,1)S(1)}, bf16[8,32,384]{2,1,0:T(8,128)(2,1)S(1)}, u32[]{:S(2)}, u32[]{:S(2)}) collective-permute-start(bf16[8,32,384]{2,1,0:T(8,128)(2,1)S(1)} %all_to_all.15.own0), channel_id=1, source_target_pairs={{0,8},{8,16},{16,24},{24,0},{1,9},{9,17},{17,25},{25,1},{2,10},{10... | collective-permute-start | bytes 589832 | tf_op jit(solution)/shard_map/ppermute | solution.py:28
  48.1 5.8 %collective-permute-done.6.own2 = bf16[8,32,384]{2,1,0:T(8,128)(2,1)S(1)} collective-permute-done((bf16[8,32,384]{2,1,0:T(8,128)(2,1)S(1)}, bf16[8,32,384]{2,1,0:T(8,128)(2,1)S(1)}, u32[]{:S(2)}, u32[]{:S(2)}) %collective-permute-start.6) | collective-permute-done | bytes 196640 | tf_op jit(solution)/shard_map/ppermute | solution.py:28
  53.9 1.7 %collective-permute-done.7.own3 = bf16[8,32,384]{2,1,0:T(8,128)(2,1)S(1)} collective-permute-done((bf16[8,32,384]{2,1,0:T(8,128)(2,1)S(1)}, bf16[8,32,384]{2,1,0:T(8,128)(2,1)S(1)}, u32[]{:S(2)}, u32[]{:S(2)}) %collective-permute-start.7) | collective-permute-done | bytes 196640 | tf_op jit(solution)/shard_map/ppermute | solution.py:28
  56.2 0.9 %collective-permute-done.11.other3 = bf16[8,32,384]{2,1,0:T(8,128)(2,1)S(1)} collective-permute-done((bf16[8,32,384]{2,1,0:T(8,128)(2,1)S(1)}, bf16[8,32,384]{2,1,0:T(8,128)(2,1)S(1)}, u32[]{:S(2)}, u32[]{:S(2)}) %collective-permute-start.11) | collective-permute-done | bytes 196640 | tf_op jit(solution)/shard_map/ppermute | solution.py:28
  57.4 1.9 %shard_map.144.p0 = bf16[32,768]{1,0:T(8,128)(2,1)S(1)} custom-call(s32[5]{0:T(128)S(1)} %stack.19.where_ref, bf16[8,32,384]{2,1,0:T(8,128)(2,1)S(1)} %all_to_all.15.own0, bf16[8,32,384]{2,1,0:T(8,128)(2,1)S(1)} %collective-permute-done.5.own1, bf16[8,32,384]{2,1,0:T(8,128)(2,1)S(1)} %collective-permute-done.6.own2, ...), custom_call_target="tpu_custom_call" | custom-call | flops 1073741824 | bytes 4194304 | tf_op jit(solution)/shard_map/pallas_call | solution.py:247
  59.3 0.9 %collective-permute-start.12 = (bf16[32,768]{1,0:T(8,128)(2,1)S(1)}, bf16[32,768]{1,0:T(8,128)(2,1)S(1)}, u32[]{:S(2)}, u32[]{:S(2)}) collective-permute-start(bf16[32,768]{1,0:T(8,128)(2,1)S(1)} %shard_map.144.p0), channel_id=1, source_target_pairs={{0,1},{1,2},{2,3},{3,0},{4,5},{5,6},{6,7},{7,4},{8,9},{9,10},{10,1... | collective-permute-start | bytes 147464 | tf_op jit(solution)/shard_map/ppermute | solution.py:28
  60.2 1.1 %collective-permute-start.13 = (bf16[32,768]{1,0:T(8,128)(2,1)S(1)}, bf16[32,768]{1,0:T(8,128)(2,1)S(1)}, u32[]{:S(2)}, u32[]{:S(2)}) collective-permute-start(bf16[32,768]{1,0:T(8,128)(2,1)S(1)} %shard_map.144.p0), channel_id=1, source_target_pairs={{0,2},{1,3},{2,0},{3,1},{4,6},{5,7},{6,4},{7,5},{8,10},{9,11},{10,... | collective-permute-start | bytes 147464 | tf_op jit(solution)/shard_map/ppermute | solution.py:28
  61.3 2.0 %collective-permute-start.14 = (bf16[32,768]{1,0:T(8,128)(2,1)S(1)}, bf16[32,768]{1,0:T(8,128)(2,1)S(1)}, u32[]{:S(2)}, u32[]{:S(2)}) collective-permute-start(bf16[32,768]{1,0:T(8,128)(2,1)S(1)} %shard_map.144.p0), channel_id=1, source_target_pairs={{0,3},{1,0},{2,1},{3,2},{4,7},{5,4},{6,5},{7,6},{8,11},{9,8},{10,9... | collective-permute-start | bytes 147464 | tf_op jit(solution)/shard_map/ppermute | solution.py:28
  63.4 1.7 %collective-permute-done.12.p1 = bf16[32,768]{1,0:T(8,128)(2,1)S(1)} collective-permute-done((bf16[32,768]{1,0:T(8,128)(2,1)S(1)}, bf16[32,768]{1,0:T(8,128)(2,1)S(1)}, u32[]{:S(2)}, u32[]{:S(2)}) %collective-permute-start.12) | collective-permute-done | bytes 49184 | tf_op jit(solution)/shard_map/ppermute | solution.py:28
  66.1 1.3 %shard_map.145 = (f32[32,192]{1,0:T(8,128)S(1)}, bf16[4,32,192]{2,1,0:T(8,128)(2,1)S(1)}) custom-call(s32[5]{0:T(128)S(1)} %stack.19.where_ref, bf16[32,768]{1,0:T(8,128)(2,1)S(1)} %shard_map.144.p0, bf16[32,768]{1,0:T(8,128)(2,1)S(1)} %collective-permute-done.12.p1, bf16[32,768]{1,0:T(8,128)(2,1)S(1)} %collective-permute-done.13.p2, ...), custom_call_target="tpu_custom_call" | custom-call | flops 1073741824 | bytes 4194304 | tf_op jit(solution)/shard_map/pallas_call | solution.py:247
  67.4 9.4 %all_to_all.16 = bf16[4,32,192]{2,1,0:T(8,128)(2,1)S(1)} all-to-all(bf16[4,32,192]{2,1,0:T(8,128)(2,1)S(1)} %get-tuple-element.30), channel_id=1, replica_groups=mesh['z'=8,'x'=4,'core'=2,'head'=4] {'head'}, dimensions={0} | all-to-all | bytes 98304 | tf_op jit(solution)/shard_map/all_to_all | solution.py:41
  (48 shorter events, 3.4 us)
Async XLA Ops:
  2.5 6.3 %collective-permute-start = (bf16[80,128]{1,0:T(8,128)(2,1)S(1)}, bf16[80,128]{1,0:T(8,128)(2,1)S(1)}, u32[]{:S(2)}, u32[]{:S(2)}) collective-permute-start(bf16[80,128]{1,0:T(8,128)(2,1)S(1)} %get-tuple-element.17.after), channel_id=1, source_target_pairs={{4,8},{12,16},{20,24},{28,32},{36,40},{44,48},{52,56},{60,64},{68,... | collective-permute-start | bytes 61448 | tf_op jit(solution)/shard_map/ppermute | solution.py:33
  4.7 4.1 %collective-permute-start.1 = (bf16[80,128]{1,0:T(8,128)(2,1)S(1)}, bf16[80,128]{1,0:T(8,128)(2,1)S(1)}, u32[]{:S(2)}, u32[]{:S(2)}) collective-permute-start(bf16[80,128]{1,0:T(8,128)(2,1)S(1)} %get-tuple-element.18), channel_id=1, source_target_pairs={{0,4},{8,12},{16,20},{24,28},{32,36},{40,44},{48,52},{56,60},{64,6... | collective-permute-start | bytes 61448 | tf_op jit(solution)/shard_map/ppermute | solution.py:33
  6.5 6.8 %copy-start.4 = (bf16[768,128]{1,0:T(8,128)(2,1)S(1)}, bf16[768,128]{1,0:T(8,128)(2,1)}, u32[]{:S(2)}) copy-start(bf16[768,128]{1,0:T(8,128)(2,1)} %atoms.1) | copy-start | bytes 589828
  6.5 6.8 %copy-start.5 = (bf16[32,768]{1,0:T(8,128)(2,1)S(1)}, bf16[32,768]{1,0:T(8,128)(2,1)}, u32[]{:S(2)}) copy-start(bf16[32,768]{1,0:T(8,128)(2,1)} %w_token.1) | copy-start | bytes 147460
  6.5 6.8 %copy-start.7 = (bf16[128,3,32]{0,2,1:T(8,128)(2,1)S(1)}, bf16[128,3,32]{0,2,1:T(8,128)(2,1)}, u32[]{:S(2)}) copy-start(bf16[128,3,32]{0,2,1:T(8,128)(2,1)} %param.17) | copy-start | bytes 73732
  8.8 17.8 %all-to-all-start = ((bf16[16,32,512]{2,1,0:T(8,128)(2,1)}), bf16[16,32,512]{2,1,0:T(8,128)(2,1)S(1)}, u32[]{:S(2)}, u32[]{:S(2)}) async-start(bf16[16,32,512]{2,1,0:T(8,128)(2,1)} %shard_map.141), calls=%async_computation | async-start | bytes 1048576 | tf_op jit(solution)/shard_map/all_to_all | solution.py:41
  13.3 8.9 %copy-start.11 = (bf16[768]{0:T(1024)(128)(2,1)S(1)}, bf16[768]{0:T(1024)(128)(2,1)}, u32[]{:S(2)}) copy-start(bf16[768]{0:T(1024)(128)(2,1)} %param.19) | copy-start | bytes 4612
  13.3 12.5 %copy-start.1 = (bf16[768,4,192]{0,2,1:T(8,128)(2,1)S(1)}, bf16[768,4,192]{0,2,1:T(8,128)(2,1)}, u32[]{:S(2)}) copy-start(bf16[768,4,192]{0,2,1:T(8,128)(2,1)} %param.20) | copy-start | bytes 3538948
  13.3 12.5 %copy-start.6 = (bf16[32,768]{1,0:T(8,128)(2,1)S(1)}, bf16[32,768]{1,0:T(8,128)(2,1)}, u32[]{:S(2)}) copy-start(bf16[32,768]{1,0:T(8,128)(2,1)} %single.1) | copy-start | bytes 147460
  16.0 8.5 %collective-permute-start.2 = (bf16[32,768]{1,0:T(8,128)(2,1)S(1)}, bf16[32,768]{1,0:T(8,128)(2,1)S(1)}, u32[]{:S(2)}, u32[]{:S(2)}) collective-permute-start(bf16[32,768]{1,0:T(8,128)(2,1)S(1)} %get-tuple-element.21.p0), channel_id=1, source_target_pairs={{0,1},{1,2},{2,3},{3,0},{4,5},{5,6},{6,7},{7,4},{8,9},{9,10},{10,1... | collective-permute-start | bytes 147464 | tf_op jit(solution)/shard_map/ppermute | solution.py:28
  18.0 7.8 %collective-permute-start.3 = (bf16[32,768]{1,0:T(8,128)(2,1)S(1)}, bf16[32,768]{1,0:T(8,128)(2,1)S(1)}, u32[]{:S(2)}, u32[]{:S(2)}) collective-permute-start(bf16[32,768]{1,0:T(8,128)(2,1)S(1)} %get-tuple-element.21.p0), channel_id=1, source_target_pairs={{0,2},{1,3},{2,0},{3,1},{4,6},{5,7},{6,4},{7,5},{8,10},{9,11},{10,... | collective-permute-start | bytes 147464 | tf_op jit(solution)/shard_map/ppermute | solution.py:28
  20.7 5.1 %collective-permute-start.4 = (bf16[32,768]{1,0:T(8,128)(2,1)S(1)}, bf16[32,768]{1,0:T(8,128)(2,1)S(1)}, u32[]{:S(2)}, u32[]{:S(2)}) collective-permute-start(bf16[32,768]{1,0:T(8,128)(2,1)S(1)} %get-tuple-element.21.p0), channel_id=1, source_target_pairs={{0,3},{1,0},{2,1},{3,2},{4,7},{5,4},{6,5},{7,6},{8,11},{9,8},{10,9... | collective-permute-start | bytes 147464 | tf_op jit(solution)/shard_map/ppermute | solution.py:28
  25.8 31.5 %copy-start.3 = (bf16[192,768]{1,0:T(8,128)(2,1)S(1)}, bf16[192,768]{1,0:T(8,128)(2,1)}, u32[]{:S(2)}) copy-start(bf16[192,768]{1,0:T(8,128)(2,1)} %w_out.1) | copy-start | bytes 884740
  44.9 9.0 %collective-permute-start.6 = (bf16[8,32,384]{2,1,0:T(8,128)(2,1)S(1)}, bf16[8,32,384]{2,1,0:T(8,128)(2,1)S(1)}, u32[]{:S(2)}, u32[]{:S(2)}) collective-permute-start(bf16[8,32,384]{2,1,0:T(8,128)(2,1)S(1)} %all_to_all.15.own0), channel_id=1, source_target_pairs={{0,16},{8,24},{16,0},{24,8},{1,17},{9,25},{17,1},{25,9},{2,18},{10... | collective-permute-start | bytes 589832 | tf_op jit(solution)/shard_map/ppermute | solution.py:28
  44.9 10.7 %collective-permute-start.7 = (bf16[8,32,384]{2,1,0:T(8,128)(2,1)S(1)}, bf16[8,32,384]{2,1,0:T(8,128)(2,1)S(1)}, u32[]{:S(2)}, u32[]{:S(2)}) collective-permute-start(bf16[8,32,384]{2,1,0:T(8,128)(2,1)S(1)} %all_to_all.15.own0), channel_id=1, source_target_pairs={{0,24},{8,0},{16,8},{24,16},{1,25},{9,1},{17,9},{25,17},{2,26},{10... | collective-permute-start | bytes 589832 | tf_op jit(solution)/shard_map/ppermute | solution.py:28
  47.0 8.6 %collective-permute-start.5 = (bf16[8,32,384]{2,1,0:T(8,128)(2,1)S(1)}, bf16[8,32,384]{2,1,0:T(8,128)(2,1)S(1)}, u32[]{:S(2)}, u32[]{:S(2)}) collective-permute-start(bf16[8,32,384]{2,1,0:T(8,128)(2,1)S(1)} %all_to_all.15.own0), channel_id=1, source_target_pairs={{0,8},{8,16},{16,24},{24,0},{1,9},{9,17},{17,25},{25,1},{2,10},{10... | collective-permute-start | bytes 589832 | tf_op jit(solution)/shard_map/ppermute | solution.py:28
  48.1 8.0 %collective-permute-start.8 = (bf16[8,32,384]{2,1,0:T(8,128)(2,1)S(1)}, bf16[8,32,384]{2,1,0:T(8,128)(2,1)S(1)}, u32[]{:S(2)}, u32[]{:S(2)}) collective-permute-start(bf16[8,32,384]{2,1,0:T(8,128)(2,1)S(1)} %all_to_all.15.own0), channel_id=1, source_target_pairs={{0,4},{4,0},{1,5},{5,1},{2,6},{6,2},{3,7},{7,3},{8,12},{12,8},{9,1... | collective-permute-start | bytes 589832 | tf_op jit(solution)/shard_map/ppermute | solution.py:28
  53.9 2.3 %collective-permute-start.10 = (bf16[8,32,384]{2,1,0:T(8,128)(2,1)S(1)}, bf16[8,32,384]{2,1,0:T(8,128)(2,1)S(1)}, u32[]{:S(2)}, u32[]{:S(2)}) collective-permute-start(bf16[8,32,384]{2,1,0:T(8,128)(2,1)S(1)} %collective-permute-done.6.own2), channel_id=1, source_target_pairs={{0,4},{4,0},{1,5},{5,1},{2,6},{6,2},{3,7},{7,3},{8,12},{12,8},{9,1... | collective-permute-start | bytes 589832 | tf_op jit(solution)/shard_map/ppermute | solution.py:28
  55.6 1.4 %collective-permute-start.11 = (bf16[8,32,384]{2,1,0:T(8,128)(2,1)S(1)}, bf16[8,32,384]{2,1,0:T(8,128)(2,1)S(1)}, u32[]{:S(2)}, u32[]{:S(2)}) collective-permute-start(bf16[8,32,384]{2,1,0:T(8,128)(2,1)S(1)} %collective-permute-done.7.own3), channel_id=1, source_target_pairs={{0,4},{4,0},{1,5},{5,1},{2,6},{6,2},{3,7},{7,3},{8,12},{12,8},{9,1... | collective-permute-start | bytes 589832 | tf_op jit(solution)/shard_map/ppermute | solution.py:28
  55.6 1.7 %collective-permute-start.9 = (bf16[8,32,384]{2,1,0:T(8,128)(2,1)S(1)}, bf16[8,32,384]{2,1,0:T(8,128)(2,1)S(1)}, u32[]{:S(2)}, u32[]{:S(2)}) collective-permute-start(bf16[8,32,384]{2,1,0:T(8,128)(2,1)S(1)} %collective-permute-done.5.own1), channel_id=1, source_target_pairs={{0,4},{4,0},{1,5},{5,1},{2,6},{6,2},{3,7},{7,3},{8,12},{12,8},{9,1... | collective-permute-start | bytes 589832 | tf_op jit(solution)/shard_map/ppermute | solution.py:28
  59.3 6.8 %copy-start.2 = (bf16[384,768]{1,0:T(8,128)(2,1)S(1)}, bf16[384,768]{1,0:T(8,128)(2,1)}, u32[]{:S(2)}) copy-start(bf16[384,768]{1,0:T(8,128)(2,1)} %w_down.1) | copy-start | bytes 1769476
  59.3 5.9 %collective-permute-start.12 = (bf16[32,768]{1,0:T(8,128)(2,1)S(1)}, bf16[32,768]{1,0:T(8,128)(2,1)S(1)}, u32[]{:S(2)}, u32[]{:S(2)}) collective-permute-start(bf16[32,768]{1,0:T(8,128)(2,1)S(1)} %shard_map.144.p0), channel_id=1, source_target_pairs={{0,1},{1,2},{2,3},{3,0},{4,5},{5,6},{6,7},{7,4},{8,9},{9,10},{10,1... | collective-permute-start | bytes 147464 | tf_op jit(solution)/shard_map/ppermute | solution.py:28
  60.2 5.6 %collective-permute-start.13 = (bf16[32,768]{1,0:T(8,128)(2,1)S(1)}, bf16[32,768]{1,0:T(8,128)(2,1)S(1)}, u32[]{:S(2)}, u32[]{:S(2)}) collective-permute-start(bf16[32,768]{1,0:T(8,128)(2,1)S(1)} %shard_map.144.p0), channel_id=1, source_target_pairs={{0,2},{1,3},{2,0},{3,1},{4,6},{5,7},{6,4},{7,5},{8,10},{9,11},{10,... | collective-permute-start | bytes 147464 | tf_op jit(solution)/shard_map/ppermute | solution.py:28
  61.3 4.8 %collective-permute-start.14 = (bf16[32,768]{1,0:T(8,128)(2,1)S(1)}, bf16[32,768]{1,0:T(8,128)(2,1)S(1)}, u32[]{:S(2)}, u32[]{:S(2)}) collective-permute-start(bf16[32,768]{1,0:T(8,128)(2,1)S(1)} %shard_map.144.p0), channel_id=1, source_target_pairs={{0,3},{1,0},{2,1},{3,2},{4,7},{5,4},{6,5},{7,6},{8,11},{9,8},{10,9... | collective-permute-start | bytes 147464 | tf_op jit(solution)/shard_map/ppermute | solution.py:28
  (5 other events, 28.4 us)

commit v3 on v2

--- a/solution.py
+++ b/solution.py
@@ -73,7 +73,7 @@
     within[...] = jnp.where(even, tail_rows, head_rows).astype(bf16)
 
 
-def pair_kernel(pair, w_bias, after, out):
+def pair_kernel(where_ref, pair, w_bias, after, out0, out1, out2, out3, out):
     tokens, keys, channels = pair.shape
     heads = w_bias.shape[0]
     count = 8
@@ -87,6 +87,8 @@
         keyed = jnp.concatenate([pair[at + q] for q in range(count)], axis=1)
         terms = lax.dot_general(spread, keyed, NT, preferred_element_type=f32)
         out[:, at : at + count, :] = terms.reshape(heads, count, keys).astype(bf16)
+    for distance, piece in enumerate((out0, out1, out2, out3)):
+        piece[...] = out[pl.ds(4 * ((where_ref[3] + distance) % 4), 4)]
 
 
 def atom_kernel(
@@ -168,8 +170,8 @@
 
 
 def attention_kernel(
-    where_ref, own0, own1, own2, own3, other0, other1, other2, other3, query, gate, bias, w_out,
-    partial, kv, scores
+    where_ref, own0, own1, own2, own3, other0, other1, other2, other3, query, gate,
+    bias0, bias1, bias2, bias3, w_out, partial, kv, scores
 ):
     core = where_ref[2]
     groups, tokens, width = own0.shape
@@ -190,17 +192,14 @@
     lane = lax.broadcasted_iota(jnp.int32, (rows, reach), 1) - (reach - part)
     queries = jnp.where((lane >= head * size) & (lane < (head + 1) * size), spread, 0.0)
     queries = queries.astype(bf16)
-    keyed = kv[...].reshape(groups * 8 * tokens, width)
-    block = bias.shape[2]
+    block = bias0.shape[2]
     scale = size ** (-0.5)
     top = None
-    for b in range(4):
+    for b, bias in enumerate((bias0, bias1, bias2, bias3)):
+        keyed = kv[pl.ds(2 * ((where_ref[3] + 4 - b) % 4), 2)].reshape(block, width)
         s = lax.dot_general(
-            queries,
-            keyed[b * block : (b + 1) * block, width - reach :],
-            NT,
-            preferred_element_type=f32,
-        ) * scale + bias[4 * b : 4 * b + 4].reshape(rows, block).astype(f32)
+            queries, keyed[:, width - reach :], NT, preferred_element_type=f32
+        ) * scale + bias[...].reshape(rows, block).astype(f32)
         scores[b] = s
         m = jnp.max(s, axis=1, keepdims=True)
         top = m if top is None else jnp.maximum(top, m)
@@ -209,10 +208,9 @@
     for b in range(4):
         lifted = jnp.exp(scores[b] - top)
         total = total + jnp.sum(lifted, axis=1, keepdims=True)
+        keyed = kv[pl.ds(2 * ((where_ref[3] + 4 - b) % 4), 2)].reshape(block, width)
         context = context + jnp.dot(
-            lifted.astype(bf16),
-            keyed[b * block : (b + 1) * block, :part],
-            preferred_element_type=f32,
+            lifted.astype(bf16), keyed[:, :part], preferred_element_type=f32
         )
     head = lax.broadcasted_iota(jnp.int32, (rows, part), 0) // tokens
     lane = lax.broadcasted_iota(jnp.int32, (rows, part), 1)
@@ -305,16 +303,17 @@
     across = swapped(sent_across, TOK, 1)
     within = swapped(sent_within, TOK, 0)
     keys = pair.shape[1]
-    pair_term = pl.pallas_call(
+    piece = jax.ShapeDtypeStruct((4, tokens, keys), bf16)
+    bias = pl.pallas_call(
         pair_kernel,
-        out_shape=jax.ShapeDtypeStruct((H, tokens, keys), bf16),
-        in_specs=[vmem, vmem, hbm],
-        out_specs=vmem,
+        out_shape=(piece, piece, piece, piece),
+        in_specs=[pl.BlockSpec(memory_space=pltpu.SMEM), vmem, vmem, hbm],
+        out_specs=(vmem, vmem, vmem, vmem),
+        scratch_shapes=[pltpu.VMEM((H, tokens, keys), bf16)],
         compiler_params=pltpu.CompilerParams(vmem_limit_bytes=16 << 20),
         cost_estimate=pl.CostEstimate(flops=2 << 30, bytes_accessed=8 << 20, transcendentals=0),
-    )(pair, w_pair_bias.T, sent_across)
-    pair_term, across, within = lax.optimization_barrier((pair_term, across, within))
-    bias = exchanged(pair_term, "head")
+    )(where_at, pair, w_pair_bias.T, sent_across)
+    across, within, *bias = lax.optimization_barrier((across, within, *bias))
 
     width = w_atom.shape[2]
     partial, mix = call(
@@ -337,6 +336,9 @@
         2,
     )
     quarter = model // 4
+    partials = of_everyone(partial)
+    partial, *bias = lax.optimization_barrier((partial, *bias))
+    bias = [bias[0]] + [sent_around(bias[d], "head", d) for d in (1, 2, 3)]
     residual, kv, query, gate = call(
         projection_kernel,
         (
@@ -346,7 +348,7 @@
             jax.ShapeDtypeStruct((tokens, quarter), f32),
         ),
         (
-            *of_everyone(partial),
+            *partials,
             single,
             ln_gain.reshape(1, model),
             w_proj.transpose(1, 2, 0).reshape(-1, model),
@@ -354,17 +356,17 @@
         [],
         0,
     )
-    kv, bias = lax.optimization_barrier((kv, bias))
     kv_own = exchanged(kv, "z")
+    kv_own, *bias = lax.optimization_barrier((kv_own, *bias))
     kv_own = [kv_own] + [sent_around(kv_own, "x", d) for d in (1, 2, 3)]
     kv_other = [sent_around(piece, "core", 1) for piece in kv_own]
     partial = call(
         attention_kernel,
         jax.ShapeDtypeStruct((tokens, model), bf16),
-        (where_at, *kv_own, *kv_other, query, gate, bias, w_out),
+        (where_at, *kv_own, *kv_other, query, gate, *bias, w_out),
         [
             pltpu.VMEM((8, 4, 2, tokens, 2 * quarter), bf16),
-            pltpu.VMEM((4, 4 * tokens, bias.shape[2]), f32),
+            pltpu.VMEM((4, 4 * tokens, keys), f32),
         ],
         1,
     )

time: 77.6 us -> 74.2 us (0.956); the launches traced: 77.4 us -> 73.2 us
  blocking collectives: 27.7 us -> 8.28 us
  starting transfers between devices: 22.4 us -> 29.8 us
  waiting for transfers between devices: 15 us -> 22.3 us
    all_to_all x2 -> x1, blocking collectives: 27.7 us -> 8.28 us  [exchanged(): return lax.all_to_all(pieces, axis, split_axis=0, concat_axis=0, tiled=True)]
    ppermute x13 -> x16, waiting for transfers between devices: 15 us -> 21.6 us  [sent_around(): lax.ppermute(block, axis, [(i, (i + distance) % size) for i in range(size)])]
    ppermute x13 -> x16, starting transfers between devices: 13.9 us -> 18.1 us  [sent_around(): lax.ppermute(block, axis, [(i, (i + distance) % size) for i in range(size)])]
    all_to_all x1, starting transfers between devices: 4.48 us -> 7.77 us  [exchanged(): return lax.all_to_all(pieces, axis, split_axis=0, concat_axis=0, tiled=True)]
  transfers between devices with their start and end apart: 16 -> 19, of which waited for: 9 -> 12; matrix products, arithmetic and copies ran while one was open for 0% -> 0% of each run, Pallas kernels for 7% -> 3%
where the time goes in v3:
time: 74.2 us; the launch traced here: 73.2 us
  starting transfers between devices  29.8 us (40%)
  waiting for transfers between devices  22.3 us (30%)
  Pallas kernels  11 us (15%)
  blocking collectives  8.28 us (11%)
  between operations  0.84 us (1%)
    ppermute x16, waiting for transfers between devices, sent_around(): lax.ppermute(block, axis, [(i, (i + distance) % size) for i in range(size)])  21.6 us
    ppermute x16, starting transfers between devices, sent_around(): lax.ppermute(block, axis, [(i, (i + distance) % size) for i in range(size)])  18.1 us
    all_to_all x1, blocking collectives, exchanged(): return lax.all_to_all(pieces, axis, split_axis=0, concat_axis=0, tiled=True)  8.28 us
    all_to_all x1, starting transfers between devices, exchanged(): return lax.all_to_all(pieces, axis, split_axis=0, concat_axis=0, tiled=True)  7.77 us
    pallas_call x4, Pallas kernels, call(): pl.pallas_call(kernel, out_shape=out_shape, in_specs=[scalar] * smem + [v...  7.15 us
    ppermute x2, starting transfers between devices, swapped(): lax.ppermute(block, axis, [(i, i + 1) for i in low] + [(i + 1, i) for i i...  3.94 us
    pallas_call x1, Pallas kernels, shards(): pl.pallas_call(pair_kernel, out_shape=(piece, piece, piece, piece), in_sp...  2.04 us
    pallas_call x1, Pallas kernels, shards(): pl.pallas_call(halo_kernel, out_shape=(send, send), in_specs=[pl.BlockSpe...  1.78 us
  transfers between devices with their start and end apart: 19, of which 12 were waited for; matrix products, arithmetic and copies ran while one was open for 0% of the time, Pallas kernels for 3%

profile of v3, /device:TPU:6, one launch (start us, length us, event | category | flops | bytes accessed | tf_op | source)
XLA Modules:
  0.0 73.2 jit_solution(15146200242715076802)
XLA Ops:
  0.7 1.8 %shard_map.140 = (bf16[80,128]{1,0:T(8,128)(2,1)S(1)}, bf16[80,128]{1,0:T(8,128)(2,1)S(1)}) custom-call(s32[5]{0:T(128)S(1)} %stack.19.where_ref, s32[32]{0:T(128)} %count_ref.1, bf16[768,128]{1,0:T(8,128)(2,1)} %atoms.1), custom_call_target="tpu_custom_call" | custom-call | flops 8589934592 | bytes 33554432 | tf_op jit(solution)/shard_map/pallas_call | solution.py:285
  2.5 2.2 %collective-permute-start = (bf16[80,128]{1,0:T(8,128)(2,1)S(1)}, bf16[80,128]{1,0:T(8,128)(2,1)S(1)}, u32[]{:S(2)}, u32[]{:S(2)}) collective-permute-start(bf16[80,128]{1,0:T(8,128)(2,1)S(1)} %get-tuple-element.31.after), channel_id=1, source_target_pairs={{4,8},{12,16},{20,24},{28,32},{36,40},{44,48},{52,56},{60,64},{68,... | collective-permute-start | bytes 61448 | tf_op jit(solution)/shard_map/ppermute | solution.py:33
  4.7 1.8 %collective-permute-start.1 = (bf16[80,128]{1,0:T(8,128)(2,1)S(1)}, bf16[80,128]{1,0:T(8,128)(2,1)S(1)}, u32[]{:S(2)}, u32[]{:S(2)}) collective-permute-start(bf16[80,128]{1,0:T(8,128)(2,1)S(1)} %get-tuple-element.32), channel_id=1, source_target_pairs={{0,4},{8,12},{16,20},{24,28},{32,36},{40,44},{48,52},{56,60},{64,6... | collective-permute-start | bytes 61448 | tf_op jit(solution)/shard_map/ppermute | solution.py:33
  6.5 2.0 %shard_map.141 = (bf16[4,32,512]{2,1,0:T(8,128)(2,1)S(1)}, bf16[4,32,512]{2,1,0:T(8,128)(2,1)S(1)}, bf16[4,32,512]{2,1,0:T(8,128)(2,1)S(1)}, bf16[4,32,512]{2,1,0:T(8,128)(2,1)S(1)}) custom-call(s32[5]{0:T(128)S(1)} %stack.19.where_ref, bf16[32,512,128]{2,1,0:T(8,128)(2,1)S(1)} %copy-done, bf16[16,128]{1,0:T(8,128)(2,1)S(1)} %bitcast.18, ...), custom_call_target="tpu_custom_call" | custom-call | flops 2147483648 | bytes 8388608 | tf_op jit(solution)/shard_map/pallas_call | solution.py:307
  8.7 2.7 %shard_map.142 = (bf16[32,768]{1,0:T(8,128)(2,1)S(1)}, bf16[32,768]{1,0:T(8,128)(2,1)}) custom-call(s32[5]{0:T(128)S(1)} %stack.19.where_ref, s32[32]{0:T(128)S(1)} %copy-done.9, s32[1,32]{1,0:T(1,128)S(1)} %bitcast.19, bf16[768,128]{1,0:T(8,128)(2,1)S(1)} %copy-done.4, bf16[80,128]{1,0:T(8,128)(2,1)S(1)} %collective-permute-done.across, ...), custom_call_target="tpu_custom_call" | custom-call | flops 1073741824 | bytes 4194304 | tf_op jit(solution)/shard_map/pallas_call | solution.py:245
  11.3 1.6 %collective-permute-start.2 = (bf16[32,768]{1,0:T(8,128)(2,1)S(1)}, bf16[32,768]{1,0:T(8,128)(2,1)S(1)}, u32[]{:S(2)}, u32[]{:S(2)}) collective-permute-start(bf16[32,768]{1,0:T(8,128)(2,1)S(1)} %get-tuple-element.39.p0), channel_id=1, source_target_pairs={{0,1},{1,2},{2,3},{3,0},{4,5},{5,6},{6,7},{7,4},{8,9},{9,10},{10,1... | collective-permute-start | bytes 147464 | tf_op jit(solution)/shard_map/ppermute | solution.py:28
  12.9 2.9 %collective-permute-start.3 = (bf16[32,768]{1,0:T(8,128)(2,1)S(1)}, bf16[32,768]{1,0:T(8,128)(2,1)S(1)}, u32[]{:S(2)}, u32[]{:S(2)}) collective-permute-start(bf16[32,768]{1,0:T(8,128)(2,1)S(1)} %get-tuple-element.39.p0), channel_id=1, source_target_pairs={{0,2},{1,3},{2,0},{3,1},{4,6},{5,7},{6,4},{7,5},{8,10},{9,11},{10,... | collective-permute-start | bytes 147464 | tf_op jit(solution)/shard_map/ppermute | solution.py:28
  15.8 1.3 %collective-permute-start.4 = (bf16[32,768]{1,0:T(8,128)(2,1)S(1)}, bf16[32,768]{1,0:T(8,128)(2,1)S(1)}, u32[]{:S(2)}, u32[]{:S(2)}) collective-permute-start(bf16[32,768]{1,0:T(8,128)(2,1)S(1)} %get-tuple-element.39.p0), channel_id=1, source_target_pairs={{0,3},{1,0},{2,1},{3,2},{4,7},{5,4},{6,5},{7,6},{8,11},{9,8},{10,9... | collective-permute-start | bytes 147464 | tf_op jit(solution)/shard_map/ppermute | solution.py:28
  17.2 2.3 %collective-permute-done.3.p2 = bf16[32,768]{1,0:T(8,128)(2,1)S(1)} collective-permute-done((bf16[32,768]{1,0:T(8,128)(2,1)S(1)}, bf16[32,768]{1,0:T(8,128)(2,1)S(1)}, u32[]{:S(2)}, u32[]{:S(2)}) %collective-permute-start.3) | collective-permute-done | bytes 49184 | tf_op jit(solution)/shard_map/ppermute | solution.py:28
  19.9 1.3 %shard_map.143 = (f32[32,768]{1,0:T(8,128)S(1)}, bf16[8,32,384]{2,1,0:T(8,128)(2,1)}, bf16[32,192]{1,0:T(8,128)(2,1)S(1)}, f32[32,192]{1,0:T(8,128)S(1)}) custom-call(bf16[32,768]{1,0:T(8,128)(2,1)S(1)} %get-tuple-element.39.p0, bf16[32,768]{1,0:T(8,128)(2,1)S(1)} %collective-permute-done.2.p1, bf16[32,768]{1,0:T(8,128)(2,1)S(1)} %collective-permute-done.3.p2, ...), custom_call_target="tpu_custom_call" | custom-call | flops 1073741824 | bytes 4194304 | tf_op jit(solution)/shard_map/pallas_call | solution.py:245
  21.2 7.8 %all-to-all-start = ((bf16[8,32,384]{2,1,0:T(8,128)(2,1)}), bf16[8,32,384]{2,1,0:T(8,128)(2,1)S(1)}, u32[]{:S(2)}, u32[]{:S(2)}) async-start(bf16[8,32,384]{2,1,0:T(8,128)(2,1)} %get-tuple-element.40), calls=%async_computation | async-start | bytes 393216 | tf_op jit(solution)/shard_map/all_to_all | solution.py:41
  29.3 3.7 %collective-permute-start.6 = (bf16[4,32,512]{2,1,0:T(8,128)(2,1)S(1)}, bf16[4,32,512]{2,1,0:T(8,128)(2,1)S(1)}, u32[]{:S(2)}, u32[]{:S(2)}) collective-permute-start(bf16[4,32,512]{2,1,0:T(8,128)(2,1)S(1)} %get-tuple-element.47), channel_id=1, source_target_pairs={{0,2},{1,3},{2,0},{3,1},{4,6},{5,7},{6,4},{7,5},{8,10},{9,11},{10,... | collective-permute-start | bytes 393224 | tf_op jit(solution)/shard_map/ppermute | solution.py:28
  33.3 2.5 %collective-permute-done.5.bias1 = bf16[4,32,512]{2,1,0:T(8,128)(2,1)S(1)} collective-permute-done((bf16[4,32,512]{2,1,0:T(8,128)(2,1)S(1)}, bf16[4,32,512]{2,1,0:T(8,128)(2,1)S(1)}, u32[]{:S(2)}, u32[]{:S(2)}) %collective-permute-start.5) | collective-permute-done | bytes 131104 | tf_op jit(solution)/shard_map/ppermute | solution.py:28
  35.8 3.3 %collective-permute-done.6.bias2 = bf16[4,32,512]{2,1,0:T(8,128)(2,1)S(1)} collective-permute-done((bf16[4,32,512]{2,1,0:T(8,128)(2,1)S(1)}, bf16[4,32,512]{2,1,0:T(8,128)(2,1)S(1)}, u32[]{:S(2)}, u32[]{:S(2)}) %collective-permute-start.6) | collective-permute-done | bytes 131104 | tf_op jit(solution)/shard_map/ppermute | solution.py:28
  39.8 2.5 %collective-permute-start.8 = (bf16[8,32,384]{2,1,0:T(8,128)(2,1)S(1)}, bf16[8,32,384]{2,1,0:T(8,128)(2,1)S(1)}, u32[]{:S(2)}, u32[]{:S(2)}) collective-permute-start(bf16[8,32,384]{2,1,0:T(8,128)(2,1)S(1)} %all-to-all-done.own0), channel_id=1, source_target_pairs={{0,8},{8,16},{16,24},{24,0},{1,9},{9,17},{17,25},{25,1},{2,10},{10... | collective-permute-start | bytes 589832 | tf_op jit(solution)/shard_map/ppermute | solution.py:28
  43.2 5.7 %collective-permute-done.8.own1 = bf16[8,32,384]{2,1,0:T(8,128)(2,1)S(1)} collective-permute-done((bf16[8,32,384]{2,1,0:T(8,128)(2,1)S(1)}, bf16[8,32,384]{2,1,0:T(8,128)(2,1)S(1)}, u32[]{:S(2)}, u32[]{:S(2)}) %collective-permute-start.8) | collective-permute-done | bytes 196640 | tf_op jit(solution)/shard_map/ppermute | solution.py:28
  49.6 1.7 %collective-permute-done.10.own3 = bf16[8,32,384]{2,1,0:T(8,128)(2,1)S(1)} collective-permute-done((bf16[8,32,384]{2,1,0:T(8,128)(2,1)S(1)}, bf16[8,32,384]{2,1,0:T(8,128)(2,1)S(1)}, u32[]{:S(2)}, u32[]{:S(2)}) %collective-permute-start.10) | collective-permute-done | bytes 196640 | tf_op jit(solution)/shard_map/ppermute | solution.py:28
  51.3 1.4 %collective-permute-done.14.other3 = bf16[8,32,384]{2,1,0:T(8,128)(2,1)S(1)} collective-permute-done((bf16[8,32,384]{2,1,0:T(8,128)(2,1)S(1)}, bf16[8,32,384]{2,1,0:T(8,128)(2,1)S(1)}, u32[]{:S(2)}, u32[]{:S(2)}) %collective-permute-start.14) | collective-permute-done | bytes 196640 | tf_op jit(solution)/shard_map/ppermute | solution.py:28
  52.7 1.9 %shard_map.144.p0 = bf16[32,768]{1,0:T(8,128)(2,1)S(1)} custom-call(s32[5]{0:T(128)S(1)} %stack.19.where_ref, bf16[8,32,384]{2,1,0:T(8,128)(2,1)S(1)} %all-to-all-done.own0, bf16[8,32,384]{2,1,0:T(8,128)(2,1)S(1)} %collective-permute-done.8.own1, bf16[8,32,384]{2,1,0:T(8,128)(2,1)S(1)} %collective-permute-done.9.own2, ...), custom_call_target="tpu_custom_call" | custom-call | flops 1073741824 | bytes 4194304 | tf_op jit(solution)/shard_map/pallas_call | solution.py:245
  54.6 1.8 %collective-permute-start.15 = (bf16[32,768]{1,0:T(8,128)(2,1)S(1)}, bf16[32,768]{1,0:T(8,128)(2,1)S(1)}, u32[]{:S(2)}, u32[]{:S(2)}) collective-permute-start(bf16[32,768]{1,0:T(8,128)(2,1)S(1)} %shard_map.144.p0), channel_id=1, source_target_pairs={{0,1},{1,2},{2,3},{3,0},{4,5},{5,6},{6,7},{7,4},{8,9},{9,10},{10,1... | collective-permute-start | bytes 147464 | tf_op jit(solution)/shard_map/ppermute | solution.py:28
  56.5 2.4 %collective-permute-start.16 = (bf16[32,768]{1,0:T(8,128)(2,1)S(1)}, bf16[32,768]{1,0:T(8,128)(2,1)S(1)}, u32[]{:S(2)}, u32[]{:S(2)}) collective-permute-start(bf16[32,768]{1,0:T(8,128)(2,1)S(1)} %shard_map.144.p0), channel_id=1, source_target_pairs={{0,2},{1,3},{2,0},{3,1},{4,6},{5,7},{6,4},{7,5},{8,10},{9,11},{10,... | collective-permute-start | bytes 147464 | tf_op jit(solution)/shard_map/ppermute | solution.py:28
  60.0 2.0 %collective-permute-done.16.p2 = bf16[32,768]{1,0:T(8,128)(2,1)S(1)} collective-permute-done((bf16[32,768]{1,0:T(8,128)(2,1)S(1)}, bf16[32,768]{1,0:T(8,128)(2,1)S(1)}, u32[]{:S(2)}, u32[]{:S(2)}) %collective-permute-start.16) | collective-permute-done | bytes 49184 | tf_op jit(solution)/shard_map/ppermute | solution.py:28
  63.0 1.3 %shard_map.145 = (f32[32,192]{1,0:T(8,128)S(1)}, bf16[4,32,192]{2,1,0:T(8,128)(2,1)S(1)}) custom-call(s32[5]{0:T(128)S(1)} %stack.19.where_ref, bf16[32,768]{1,0:T(8,128)(2,1)S(1)} %shard_map.144.p0, bf16[32,768]{1,0:T(8,128)(2,1)S(1)} %collective-permute-done.15.p1, bf16[32,768]{1,0:T(8,128)(2,1)S(1)} %collective-permute-done.16.p2, ...), custom_call_target="tpu_custom_call" | custom-call | flops 1073741824 | bytes 4194304 | tf_op jit(solution)/shard_map/pallas_call | solution.py:245
  64.2 8.3 %all_to_all.10 = bf16[4,32,192]{2,1,0:T(8,128)(2,1)S(1)} all-to-all(bf16[4,32,192]{2,1,0:T(8,128)(2,1)S(1)} %get-tuple-element.58), channel_id=1, replica_groups=mesh['z'=8,'x'=4,'core'=2,'head'=4] {'head'}, dimensions={0} | all-to-all | bytes 98304 | tf_op jit(solution)/shard_map/all_to_all | solution.py:41
  (53 shorter events, 6.1 us)
Async XLA Ops:
  2.5 6.0 %collective-permute-start = (bf16[80,128]{1,0:T(8,128)(2,1)S(1)}, bf16[80,128]{1,0:T(8,128)(2,1)S(1)}, u32[]{:S(2)}, u32[]{:S(2)}) collective-permute-start(bf16[80,128]{1,0:T(8,128)(2,1)S(1)} %get-tuple-element.31.after), channel_id=1, source_target_pairs={{4,8},{12,16},{20,24},{28,32},{36,40},{44,48},{52,56},{60,64},{68,... | collective-permute-start | bytes 61448 | tf_op jit(solution)/shard_map/ppermute | solution.py:33
  4.7 3.9 %collective-permute-start.1 = (bf16[80,128]{1,0:T(8,128)(2,1)S(1)}, bf16[80,128]{1,0:T(8,128)(2,1)S(1)}, u32[]{:S(2)}, u32[]{:S(2)}) collective-permute-start(bf16[80,128]{1,0:T(8,128)(2,1)S(1)} %get-tuple-element.32), channel_id=1, source_target_pairs={{0,4},{8,12},{16,20},{24,28},{32,36},{40,44},{48,52},{56,60},{64,6... | collective-permute-start | bytes 61448 | tf_op jit(solution)/shard_map/ppermute | solution.py:33
  8.6 8.6 %copy-start.11 = (bf16[768]{0:T(1024)(128)(2,1)S(1)}, bf16[768]{0:T(1024)(128)(2,1)}, u32[]{:S(2)}) copy-start(bf16[768]{0:T(1024)(128)(2,1)} %param.19) | copy-start | bytes 4612
  8.6 11.3 %copy-start.1 = (bf16[768,4,192]{0,2,1:T(8,128)(2,1)S(1)}, bf16[768,4,192]{0,2,1:T(8,128)(2,1)}, u32[]{:S(2)}) copy-start(bf16[768,4,192]{0,2,1:T(8,128)(2,1)} %param.20) | copy-start | bytes 3538948
  8.6 11.3 %copy-start.6 = (bf16[32,768]{1,0:T(8,128)(2,1)S(1)}, bf16[32,768]{1,0:T(8,128)(2,1)}, u32[]{:S(2)}) copy-start(bf16[32,768]{1,0:T(8,128)(2,1)} %single.1) | copy-start | bytes 147460
  11.3 5.8 %collective-permute-start.2 = (bf16[32,768]{1,0:T(8,128)(2,1)S(1)}, bf16[32,768]{1,0:T(8,128)(2,1)S(1)}, u32[]{:S(2)}, u32[]{:S(2)}) collective-permute-start(bf16[32,768]{1,0:T(8,128)(2,1)S(1)} %get-tuple-element.39.p0), channel_id=1, source_target_pairs={{0,1},{1,2},{2,3},{3,0},{4,5},{5,6},{6,7},{7,4},{8,9},{9,10},{10,1... | collective-permute-start | bytes 147464 | tf_op jit(solution)/shard_map/ppermute | solution.py:28
  12.9 6.5 %collective-permute-start.3 = (bf16[32,768]{1,0:T(8,128)(2,1)S(1)}, bf16[32,768]{1,0:T(8,128)(2,1)S(1)}, u32[]{:S(2)}, u32[]{:S(2)}) collective-permute-start(bf16[32,768]{1,0:T(8,128)(2,1)S(1)} %get-tuple-element.39.p0), channel_id=1, source_target_pairs={{0,2},{1,3},{2,0},{3,1},{4,6},{5,7},{6,4},{7,5},{8,10},{9,11},{10,... | collective-permute-start | bytes 147464 | tf_op jit(solution)/shard_map/ppermute | solution.py:28
  15.8 4.1 %collective-permute-start.4 = (bf16[32,768]{1,0:T(8,128)(2,1)S(1)}, bf16[32,768]{1,0:T(8,128)(2,1)S(1)}, u32[]{:S(2)}, u32[]{:S(2)}) collective-permute-start(bf16[32,768]{1,0:T(8,128)(2,1)S(1)} %get-tuple-element.39.p0), channel_id=1, source_target_pairs={{0,3},{1,0},{2,1},{3,2},{4,7},{5,4},{6,5},{7,6},{8,11},{9,8},{10,9... | collective-permute-start | bytes 147464 | tf_op jit(solution)/shard_map/ppermute | solution.py:28
  19.9 32.8 %copy-start.3 = (bf16[192,768]{1,0:T(8,128)(2,1)S(1)}, bf16[192,768]{1,0:T(8,128)(2,1)}, u32[]{:S(2)}) copy-start(bf16[192,768]{1,0:T(8,128)(2,1)} %w_out.1) | copy-start | bytes 884740
  21.2 18.6 %all-to-all-start = ((bf16[8,32,384]{2,1,0:T(8,128)(2,1)}), bf16[8,32,384]{2,1,0:T(8,128)(2,1)S(1)}, u32[]{:S(2)}, u32[]{:S(2)}) async-start(bf16[8,32,384]{2,1,0:T(8,128)(2,1)} %get-tuple-element.40), calls=%async_computation | async-start | bytes 393216 | tf_op jit(solution)/shard_map/all_to_all | solution.py:41
  29.0 6.8 %collective-permute-start.5 = (bf16[4,32,512]{2,1,0:T(8,128)(2,1)S(1)}, bf16[4,32,512]{2,1,0:T(8,128)(2,1)S(1)}, u32[]{:S(2)}, u32[]{:S(2)}) collective-permute-start(bf16[4,32,512]{2,1,0:T(8,128)(2,1)S(1)} %get-tuple-element.46), channel_id=1, source_target_pairs={{0,1},{1,2},{2,3},{3,0},{4,5},{5,6},{6,7},{7,4},{8,9},{9,10},{10,1... | collective-permute-start | bytes 393224 | tf_op jit(solution)/shard_map/ppermute | solution.py:28
  29.3 9.8 %collective-permute-start.6 = (bf16[4,32,512]{2,1,0:T(8,128)(2,1)S(1)}, bf16[4,32,512]{2,1,0:T(8,128)(2,1)S(1)}, u32[]{:S(2)}, u32[]{:S(2)}) collective-permute-start(bf16[4,32,512]{2,1,0:T(8,128)(2,1)S(1)} %get-tuple-element.47), channel_id=1, source_target_pairs={{0,2},{1,3},{2,0},{3,1},{4,6},{5,7},{6,4},{7,5},{8,10},{9,11},{10,... | collective-permute-start | bytes 393224 | tf_op jit(solution)/shard_map/ppermute | solution.py:28
  33.0 6.1 %collective-permute-start.7 = (bf16[4,32,512]{2,1,0:T(8,128)(2,1)S(1)}, bf16[4,32,512]{2,1,0:T(8,128)(2,1)S(1)}, u32[]{:S(2)}, u32[]{:S(2)}) collective-permute-start(bf16[4,32,512]{2,1,0:T(8,128)(2,1)S(1)} %get-tuple-element.48), channel_id=1, source_target_pairs={{0,3},{1,0},{2,1},{3,2},{4,7},{5,4},{6,5},{7,6},{8,11},{9,8},{10,9... | collective-permute-start | bytes 393224 | tf_op jit(solution)/shard_map/ppermute | solution.py:28
  39.8 9.1 %collective-permute-start.8 = (bf16[8,32,384]{2,1,0:T(8,128)(2,1)S(1)}, bf16[8,32,384]{2,1,0:T(8,128)(2,1)S(1)}, u32[]{:S(2)}, u32[]{:S(2)}) collective-permute-start(bf16[8,32,384]{2,1,0:T(8,128)(2,1)S(1)} %all-to-all-done.own0), channel_id=1, source_target_pairs={{0,8},{8,16},{16,24},{24,0},{1,9},{9,17},{17,25},{25,1},{2,10},{10... | collective-permute-start | bytes 589832 | tf_op jit(solution)/shard_map/ppermute | solution.py:28
  42.3 7.3 %collective-permute-start.9 = (bf16[8,32,384]{2,1,0:T(8,128)(2,1)S(1)}, bf16[8,32,384]{2,1,0:T(8,128)(2,1)S(1)}, u32[]{:S(2)}, u32[]{:S(2)}) collective-permute-start(bf16[8,32,384]{2,1,0:T(8,128)(2,1)S(1)} %all-to-all-done.own0), channel_id=1, source_target_pairs={{0,16},{8,24},{16,0},{24,8},{1,17},{9,25},{17,1},{25,9},{2,18},{10... | collective-permute-start | bytes 589832 | tf_op jit(solution)/shard_map/ppermute | solution.py:28
  42.3 9.0 %collective-permute-start.10 = (bf16[8,32,384]{2,1,0:T(8,128)(2,1)S(1)}, bf16[8,32,384]{2,1,0:T(8,128)(2,1)S(1)}, u32[]{:S(2)}, u32[]{:S(2)}) collective-permute-start(bf16[8,32,384]{2,1,0:T(8,128)(2,1)S(1)} %all-to-all-done.own0), channel_id=1, source_target_pairs={{0,24},{8,0},{16,8},{24,16},{1,25},{9,1},{17,9},{25,17},{2,26},{10... | collective-permute-start | bytes 589832 | tf_op jit(solution)/shard_map/ppermute | solution.py:28
  43.2 8.1 %collective-permute-start.11 = (bf16[8,32,384]{2,1,0:T(8,128)(2,1)S(1)}, bf16[8,32,384]{2,1,0:T(8,128)(2,1)S(1)}, u32[]{:S(2)}, u32[]{:S(2)}) collective-permute-start(bf16[8,32,384]{2,1,0:T(8,128)(2,1)S(1)} %all-to-all-done.own0), channel_id=1, source_target_pairs={{0,4},{4,0},{1,5},{5,1},{2,6},{6,2},{3,7},{7,3},{8,12},{12,8},{9,1... | collective-permute-start | bytes 589832 | tf_op jit(solution)/shard_map/ppermute | solution.py:28
  48.9 2.4 %collective-permute-start.12 = (bf16[8,32,384]{2,1,0:T(8,128)(2,1)S(1)}, bf16[8,32,384]{2,1,0:T(8,128)(2,1)S(1)}, u32[]{:S(2)}, u32[]{:S(2)}) collective-permute-start(bf16[8,32,384]{2,1,0:T(8,128)(2,1)S(1)} %collective-permute-done.8.own1), channel_id=1, source_target_pairs={{0,4},{4,0},{1,5},{5,1},{2,6},{6,2},{3,7},{7,3},{8,12},{12,8},{9,1... | collective-permute-start | bytes 589832 | tf_op jit(solution)/shard_map/ppermute | solution.py:28
  49.6 1.7 %collective-permute-start.13 = (bf16[8,32,384]{2,1,0:T(8,128)(2,1)S(1)}, bf16[8,32,384]{2,1,0:T(8,128)(2,1)S(1)}, u32[]{:S(2)}, u32[]{:S(2)}) collective-permute-start(bf16[8,32,384]{2,1,0:T(8,128)(2,1)S(1)} %collective-permute-done.9.own2), channel_id=1, source_target_pairs={{0,4},{4,0},{1,5},{5,1},{2,6},{6,2},{3,7},{7,3},{8,12},{12,8},{9,1... | collective-permute-start | bytes 589832 | tf_op jit(solution)/shard_map/ppermute | solution.py:28
  51.3 1.4 %collective-permute-start.14 = (bf16[8,32,384]{2,1,0:T(8,128)(2,1)S(1)}, bf16[8,32,384]{2,1,0:T(8,128)(2,1)S(1)}, u32[]{:S(2)}, u32[]{:S(2)}) collective-permute-start(bf16[8,32,384]{2,1,0:T(8,128)(2,1)S(1)} %collective-permute-done.10.own3), channel_id=1, source_target_pairs={{0,4},{4,0},{1,5},{5,1},{2,6},{6,2},{3,7},{7,3},{8,12},{12,8},{9,1... | collective-permute-start | bytes 589832 | tf_op jit(solution)/shard_map/ppermute | solution.py:28
  54.6 8.3 %copy-start.2 = (bf16[384,768]{1,0:T(8,128)(2,1)S(1)}, bf16[384,768]{1,0:T(8,128)(2,1)}, u32[]{:S(2)}) copy-start(bf16[384,768]{1,0:T(8,128)(2,1)} %w_down.1) | copy-start | bytes 1769476
  54.6 5.4 %collective-permute-start.15 = (bf16[32,768]{1,0:T(8,128)(2,1)S(1)}, bf16[32,768]{1,0:T(8,128)(2,1)S(1)}, u32[]{:S(2)}, u32[]{:S(2)}) collective-permute-start(bf16[32,768]{1,0:T(8,128)(2,1)S(1)} %shard_map.144.p0), channel_id=1, source_target_pairs={{0,1},{1,2},{2,3},{3,0},{4,5},{5,6},{6,7},{7,4},{8,9},{9,10},{10,1... | collective-permute-start | bytes 147464 | tf_op jit(solution)/shard_map/ppermute | solution.py:28
  56.5 5.6 %collective-permute-start.16 = (bf16[32,768]{1,0:T(8,128)(2,1)S(1)}, bf16[32,768]{1,0:T(8,128)(2,1)S(1)}, u32[]{:S(2)}, u32[]{:S(2)}) collective-permute-start(bf16[32,768]{1,0:T(8,128)(2,1)S(1)} %shard_map.144.p0), channel_id=1, source_target_pairs={{0,2},{1,3},{2,0},{3,1},{4,6},{5,7},{6,4},{7,5},{8,10},{9,11},{10,... | collective-permute-start | bytes 147464 | tf_op jit(solution)/shard_map/ppermute | solution.py:28
  58.9 4.1 %collective-permute-start.17 = (bf16[32,768]{1,0:T(8,128)(2,1)S(1)}, bf16[32,768]{1,0:T(8,128)(2,1)S(1)}, u32[]{:S(2)}, u32[]{:S(2)}) collective-permute-start(bf16[32,768]{1,0:T(8,128)(2,1)S(1)} %shard_map.144.p0), channel_id=1, source_target_pairs={{0,3},{1,0},{2,1},{3,2},{4,7},{5,4},{6,5},{7,6},{8,11},{9,8},{10,9... | collective-permute-start | bytes 147464 | tf_op jit(solution)/shard_map/ppermute | solution.py:28
  (8 other events, 31.2 us)

commit v4 on v3

--- a/solution.py
+++ b/solution.py
@@ -222,21 +222,25 @@
 
 
 def tail_kernel(
-    where_ref, p0, p1, p2, p3, residual, gain, w_trans, w_down, share, update, state
+    where_ref, p0, p1, p2, p3, residual, gain, w_trans, w_down, share, update1, update2, update3, state,
+    moved_rows
 ):
     term = (p0[...].astype(f32) + p1[...].astype(f32)) + (p2[...].astype(f32) + p3[...].astype(f32))
     after = residual[...] + term
     quarter = share.shape[1]
     for y in range(4):
         state[y] = after[:, y * quarter : (y + 1) * quarter]
-    share[...] = state[where_ref[3]]
     normed = layer_norm(after, gain[...].astype(f32)).astype(bf16)
     gate = jnp.dot(normed, w_trans[0], preferred_element_type=f32)
     up = jnp.dot(normed, w_trans[1], preferred_element_type=f32)
     hidden = (gate * jax.nn.sigmoid(gate) * up).astype(bf16)
     moved = jnp.dot(hidden, w_down[...], preferred_element_type=f32)
     for y in range(4):
-        update[y] = moved[:, y * quarter : (y + 1) * quarter].astype(bf16)
+        moved_rows[y] = moved[:, y * quarter : (y + 1) * quarter]
+    head = where_ref[3]
+    share[...] = state[head] + moved_rows[head]
+    for distance, update in ((1, update1), (2, update2), (3, update3)):
+        update[...] = moved_rows[(head + distance) % 4].astype(bf16)
 
 
 def call(kernel, out_shape, operands, scratch, smem):
@@ -370,11 +374,11 @@
         ],
         1,
     )
-    share, update = call(
+    share, *updates = call(
         tail_kernel,
         (
             jax.ShapeDtypeStruct((tokens, quarter), f32),
-            jax.ShapeDtypeStruct((4, tokens, quarter), bf16),
+            *[jax.ShapeDtypeStruct((tokens, quarter), bf16) for _ in range(3)],
         ),
         (
             where_at,
@@ -384,11 +388,11 @@
             w_trans.transpose(1, 0, 2),
             w_trans_out,
         ),
-        [pltpu.VMEM((4, tokens, quarter), f32)],
+        [pltpu.VMEM((4, tokens, quarter), f32), pltpu.VMEM((4, tokens, quarter), f32)],
         1,
     )
-    update = exchanged(update, "head")
-    refined = (share + update.astype(f32).sum(axis=0)).astype(bf16)
+    updates = [sent_around(u, "head", d) for u, d in zip(updates, (1, 2, 3))]
+    refined = (share + sum(u.astype(f32) for u in updates)).astype(bf16)
     return (refined, mix)
 
 

time: 74.2 us -> 73.1 us (0.985)
  blocking collectives: 8.28 us -> 0 us
  starting transfers between devices: 29.8 us -> 34 us
  waiting for transfers between devices: 22.3 us -> 25 us
    all_to_all x1 -> x0, blocking collectives: 8.28 us -> none  [exchanged(): return lax.all_to_all(pieces, axis, split_axis=0, concat_axis=0, tiled=True)]
    ppermute x16 -> x19, starting transfers between devices: 18.1 us -> 22.3 us  [sent_around(): lax.ppermute(block, axis, [(i, (i + distance) % size) for i in range(size)])]
    ppermute x16 -> x19, waiting for transfers between devices: 21.6 us -> 24.3 us  [sent_around(): lax.ppermute(block, axis, [(i, (i + distance) % size) for i in range(size)])]
  transfers between devices with their start and end apart: 19 -> 22, of which waited for: 12 -> 15; matrix products, arithmetic and copies ran while one was open for 0% -> 0% of each run, Pallas kernels for 3% -> 3%
where the time goes in v4:
time: 73.1 us; the launch traced here: 71.7 us
  starting transfers between devices  34 us (47%)
  waiting for transfers between devices  25 us (34%)
  Pallas kernels  11 us (15%)
  between operations  0.85 us (1%)
    ppermute x19, waiting for transfers between devices, sent_around(): lax.ppermute(block, axis, [(i, (i + distance) % size) for i in range(size)])  24.3 us
    ppermute x19, starting transfers between devices, sent_around(): lax.ppermute(block, axis, [(i, (i + distance) % size) for i in range(size)])  22.3 us
    all_to_all x1, starting transfers between devices, exchanged(): return lax.all_to_all(pieces, axis, split_axis=0, concat_axis=0, tiled=True)  7.77 us
    pallas_call x4, Pallas kernels, call(): pl.pallas_call(kernel, out_shape=out_shape, in_specs=[scalar] * smem + [v...  7.16 us
    ppermute x2, starting transfers between devices, swapped(): lax.ppermute(block, axis, [(i, i + 1) for i in low] + [(i + 1, i) for i i...  3.94 us
    pallas_call x1, Pallas kernels, shards(): pl.pallas_call(pair_kernel, out_shape=(piece, piece, piece, piece), in_sp...  2.04 us
    pallas_call x1, Pallas kernels, shards(): pl.pallas_call(halo_kernel, out_shape=(send, send), in_specs=[pl.BlockSpe...  1.79 us
  transfers between devices with their start and end apart: 22, of which 15 were waited for; matrix products, arithmetic and copies ran while one was open for 0% of the time, Pallas kernels for 3%

profile of v4, /device:TPU:6, one launch (start us, length us, event | category | flops | bytes accessed | tf_op | source)
XLA Modules:
  0.0 71.7 jit_solution(9982259222026307998)
XLA Ops:
  0.7 1.8 %shard_map.140 = (bf16[80,128]{1,0:T(8,128)(2,1)S(1)}, bf16[80,128]{1,0:T(8,128)(2,1)S(1)}) custom-call(s32[5]{0:T(128)S(1)} %stack.19.where_ref, s32[32]{0:T(128)} %count_ref.1, bf16[768,128]{1,0:T(8,128)(2,1)} %atoms.1), custom_call_target="tpu_custom_call" | custom-call | flops 8589934592 | bytes 33554432 | tf_op jit(solution)/shard_map/pallas_call | solution.py:289
  2.5 2.2 %collective-permute-start = (bf16[80,128]{1,0:T(8,128)(2,1)S(1)}, bf16[80,128]{1,0:T(8,128)(2,1)S(1)}, u32[]{:S(2)}, u32[]{:S(2)}) collective-permute-start(bf16[80,128]{1,0:T(8,128)(2,1)S(1)} %get-tuple-element.33.after), channel_id=1, source_target_pairs={{4,8},{12,16},{20,24},{28,32},{36,40},{44,48},{52,56},{60,64},{68,... | collective-permute-start | bytes 61448 | tf_op jit(solution)/shard_map/ppermute | solution.py:33
  4.7 1.8 %collective-permute-start.1 = (bf16[80,128]{1,0:T(8,128)(2,1)S(1)}, bf16[80,128]{1,0:T(8,128)(2,1)S(1)}, u32[]{:S(2)}, u32[]{:S(2)}) collective-permute-start(bf16[80,128]{1,0:T(8,128)(2,1)S(1)} %get-tuple-element.34), channel_id=1, source_target_pairs={{0,4},{8,12},{16,20},{24,28},{32,36},{40,44},{48,52},{56,60},{64,6... | collective-permute-start | bytes 61448 | tf_op jit(solution)/shard_map/ppermute | solution.py:33
  6.5 2.0 %shard_map.141 = (bf16[4,32,512]{2,1,0:T(8,128)(2,1)S(1)}, bf16[4,32,512]{2,1,0:T(8,128)(2,1)S(1)}, bf16[4,32,512]{2,1,0:T(8,128)(2,1)S(1)}, bf16[4,32,512]{2,1,0:T(8,128)(2,1)S(1)}) custom-call(s32[5]{0:T(128)S(1)} %stack.19.where_ref, bf16[32,512,128]{2,1,0:T(8,128)(2,1)S(1)} %copy-done, bf16[16,128]{1,0:T(8,128)(2,1)S(1)} %bitcast.18, ...), custom_call_target="tpu_custom_call" | custom-call | flops 2147483648 | bytes 8388608 | tf_op jit(solution)/shard_map/pallas_call | solution.py:311
  8.7 2.7 %shard_map.142 = (bf16[32,768]{1,0:T(8,128)(2,1)S(1)}, bf16[32,768]{1,0:T(8,128)(2,1)}) custom-call(s32[5]{0:T(128)S(1)} %stack.19.where_ref, s32[32]{0:T(128)S(1)} %copy-done.9, s32[1,32]{1,0:T(1,128)S(1)} %bitcast.19, bf16[768,128]{1,0:T(8,128)(2,1)S(1)} %copy-done.4, bf16[80,128]{1,0:T(8,128)(2,1)S(1)} %collective-permute-done.across, ...), custom_call_target="tpu_custom_call" | custom-call | flops 1073741824 | bytes 4194304 | tf_op jit(solution)/shard_map/pallas_call | solution.py:249
  11.3 1.6 %collective-permute-start.2 = (bf16[32,768]{1,0:T(8,128)(2,1)S(1)}, bf16[32,768]{1,0:T(8,128)(2,1)S(1)}, u32[]{:S(2)}, u32[]{:S(2)}) collective-permute-start(bf16[32,768]{1,0:T(8,128)(2,1)S(1)} %get-tuple-element.41.p0), channel_id=1, source_target_pairs={{0,1},{1,2},{2,3},{3,0},{4,5},{5,6},{6,7},{7,4},{8,9},{9,10},{10,1... | collective-permute-start | bytes 147464 | tf_op jit(solution)/shard_map/ppermute | solution.py:28
  12.9 2.9 %collective-permute-start.3 = (bf16[32,768]{1,0:T(8,128)(2,1)S(1)}, bf16[32,768]{1,0:T(8,128)(2,1)S(1)}, u32[]{:S(2)}, u32[]{:S(2)}) collective-permute-start(bf16[32,768]{1,0:T(8,128)(2,1)S(1)} %get-tuple-element.41.p0), channel_id=1, source_target_pairs={{0,2},{1,3},{2,0},{3,1},{4,6},{5,7},{6,4},{7,5},{8,10},{9,11},{10,... | collective-permute-start | bytes 147464 | tf_op jit(solution)/shard_map/ppermute | solution.py:28
  15.8 1.3 %collective-permute-start.4 = (bf16[32,768]{1,0:T(8,128)(2,1)S(1)}, bf16[32,768]{1,0:T(8,128)(2,1)S(1)}, u32[]{:S(2)}, u32[]{:S(2)}) collective-permute-start(bf16[32,768]{1,0:T(8,128)(2,1)S(1)} %get-tuple-element.41.p0), channel_id=1, source_target_pairs={{0,3},{1,0},{2,1},{3,2},{4,7},{5,4},{6,5},{7,6},{8,11},{9,8},{10,9... | collective-permute-start | bytes 147464 | tf_op jit(solution)/shard_map/ppermute | solution.py:28
  17.2 2.3 %collective-permute-done.3.p2 = bf16[32,768]{1,0:T(8,128)(2,1)S(1)} collective-permute-done((bf16[32,768]{1,0:T(8,128)(2,1)S(1)}, bf16[32,768]{1,0:T(8,128)(2,1)S(1)}, u32[]{:S(2)}, u32[]{:S(2)}) %collective-permute-start.3) | collective-permute-done | bytes 49184 | tf_op jit(solution)/shard_map/ppermute | solution.py:28
  19.9 1.3 %shard_map.143 = (f32[32,768]{1,0:T(8,128)S(1)}, bf16[8,32,384]{2,1,0:T(8,128)(2,1)}, bf16[32,192]{1,0:T(8,128)(2,1)S(1)}, f32[32,192]{1,0:T(8,128)S(1)}) custom-call(bf16[32,768]{1,0:T(8,128)(2,1)S(1)} %get-tuple-element.41.p0, bf16[32,768]{1,0:T(8,128)(2,1)S(1)} %collective-permute-done.2.p1, bf16[32,768]{1,0:T(8,128)(2,1)S(1)} %collective-permute-done.3.p2, ...), custom_call_target="tpu_custom_call" | custom-call | flops 1073741824 | bytes 4194304 | tf_op jit(solution)/shard_map/pallas_call | solution.py:249
  21.2 7.8 %all-to-all-start = ((bf16[8,32,384]{2,1,0:T(8,128)(2,1)}), bf16[8,32,384]{2,1,0:T(8,128)(2,1)S(1)}, u32[]{:S(2)}, u32[]{:S(2)}) async-start(bf16[8,32,384]{2,1,0:T(8,128)(2,1)} %get-tuple-element.42), calls=%async_computation | async-start | bytes 393216 | tf_op jit(solution)/shard_map/all_to_all | solution.py:41
  29.3 3.7 %collective-permute-start.6 = (bf16[4,32,512]{2,1,0:T(8,128)(2,1)S(1)}, bf16[4,32,512]{2,1,0:T(8,128)(2,1)S(1)}, u32[]{:S(2)}, u32[]{:S(2)}) collective-permute-start(bf16[4,32,512]{2,1,0:T(8,128)(2,1)S(1)} %get-tuple-element.49), channel_id=1, source_target_pairs={{0,2},{1,3},{2,0},{3,1},{4,6},{5,7},{6,4},{7,5},{8,10},{9,11},{10,... | collective-permute-start | bytes 393224 | tf_op jit(solution)/shard_map/ppermute | solution.py:28
  33.3 2.5 %collective-permute-done.5.bias1 = bf16[4,32,512]{2,1,0:T(8,128)(2,1)S(1)} collective-permute-done((bf16[4,32,512]{2,1,0:T(8,128)(2,1)S(1)}, bf16[4,32,512]{2,1,0:T(8,128)(2,1)S(1)}, u32[]{:S(2)}, u32[]{:S(2)}) %collective-permute-start.5) | collective-permute-done | bytes 131104 | tf_op jit(solution)/shard_map/ppermute | solution.py:28
  35.8 3.3 %collective-permute-done.6.bias2 = bf16[4,32,512]{2,1,0:T(8,128)(2,1)S(1)} collective-permute-done((bf16[4,32,512]{2,1,0:T(8,128)(2,1)S(1)}, bf16[4,32,512]{2,1,0:T(8,128)(2,1)S(1)}, u32[]{:S(2)}, u32[]{:S(2)}) %collective-permute-start.6) | collective-permute-done | bytes 131104 | tf_op jit(solution)/shard_map/ppermute | solution.py:28
  39.8 2.5 %collective-permute-start.8 = (bf16[8,32,384]{2,1,0:T(8,128)(2,1)S(1)}, bf16[8,32,384]{2,1,0:T(8,128)(2,1)S(1)}, u32[]{:S(2)}, u32[]{:S(2)}) collective-permute-start(bf16[8,32,384]{2,1,0:T(8,128)(2,1)S(1)} %all-to-all-done.own0), channel_id=1, source_target_pairs={{0,8},{8,16},{16,24},{24,0},{1,9},{9,17},{17,25},{25,1},{2,10},{10... | collective-permute-start | bytes 589832 | tf_op jit(solution)/shard_map/ppermute | solution.py:28
  43.2 5.7 %collective-permute-done.8.own1 = bf16[8,32,384]{2,1,0:T(8,128)(2,1)S(1)} collective-permute-done((bf16[8,32,384]{2,1,0:T(8,128)(2,1)S(1)}, bf16[8,32,384]{2,1,0:T(8,128)(2,1)S(1)}, u32[]{:S(2)}, u32[]{:S(2)}) %collective-permute-start.8) | collective-permute-done | bytes 196640 | tf_op jit(solution)/shard_map/ppermute | solution.py:28
  49.6 1.7 %collective-permute-done.10.own3 = bf16[8,32,384]{2,1,0:T(8,128)(2,1)S(1)} collective-permute-done((bf16[8,32,384]{2,1,0:T(8,128)(2,1)S(1)}, bf16[8,32,384]{2,1,0:T(8,128)(2,1)S(1)}, u32[]{:S(2)}, u32[]{:S(2)}) %collective-permute-start.10) | collective-permute-done | bytes 196640 | tf_op jit(solution)/shard_map/ppermute | solution.py:28
  51.3 1.4 %collective-permute-done.14.other3 = bf16[8,32,384]{2,1,0:T(8,128)(2,1)S(1)} collective-permute-done((bf16[8,32,384]{2,1,0:T(8,128)(2,1)S(1)}, bf16[8,32,384]{2,1,0:T(8,128)(2,1)S(1)}, u32[]{:S(2)}, u32[]{:S(2)}) %collective-permute-start.14) | collective-permute-done | bytes 196640 | tf_op jit(solution)/shard_map/ppermute | solution.py:28
  52.7 1.9 %shard_map.144.p0 = bf16[32,768]{1,0:T(8,128)(2,1)S(1)} custom-call(s32[5]{0:T(128)S(1)} %stack.19.where_ref, bf16[8,32,384]{2,1,0:T(8,128)(2,1)S(1)} %all-to-all-done.own0, bf16[8,32,384]{2,1,0:T(8,128)(2,1)S(1)} %collective-permute-done.8.own1, bf16[8,32,384]{2,1,0:T(8,128)(2,1)S(1)} %collective-permute-done.9.own2, ...), custom_call_target="tpu_custom_call" | custom-call | flops 1073741824 | bytes 4194304 | tf_op jit(solution)/shard_map/pallas_call | solution.py:249
  54.6 1.8 %collective-permute-start.15 = (bf16[32,768]{1,0:T(8,128)(2,1)S(1)}, bf16[32,768]{1,0:T(8,128)(2,1)S(1)}, u32[]{:S(2)}, u32[]{:S(2)}) collective-permute-start(bf16[32,768]{1,0:T(8,128)(2,1)S(1)} %shard_map.144.p0), channel_id=1, source_target_pairs={{0,1},{1,2},{2,3},{3,0},{4,5},{5,6},{6,7},{7,4},{8,9},{9,10},{10,1... | collective-permute-start | bytes 147464 | tf_op jit(solution)/shard_map/ppermute | solution.py:28
  56.5 2.4 %collective-permute-start.16 = (bf16[32,768]{1,0:T(8,128)(2,1)S(1)}, bf16[32,768]{1,0:T(8,128)(2,1)S(1)}, u32[]{:S(2)}, u32[]{:S(2)}) collective-permute-start(bf16[32,768]{1,0:T(8,128)(2,1)S(1)} %shard_map.144.p0), channel_id=1, source_target_pairs={{0,2},{1,3},{2,0},{3,1},{4,6},{5,7},{6,4},{7,5},{8,10},{9,11},{10,... | collective-permute-start | bytes 147464 | tf_op jit(solution)/shard_map/ppermute | solution.py:28
  60.0 2.0 %collective-permute-done.16.p2 = bf16[32,768]{1,0:T(8,128)(2,1)S(1)} collective-permute-done((bf16[32,768]{1,0:T(8,128)(2,1)S(1)}, bf16[32,768]{1,0:T(8,128)(2,1)S(1)}, u32[]{:S(2)}, u32[]{:S(2)}) %collective-permute-start.16) | collective-permute-done | bytes 49184 | tf_op jit(solution)/shard_map/ppermute | solution.py:28
  64.4 2.9 %collective-permute-start.19 = (bf16[32,192]{1,0:T(8,128)(2,1)S(1)}, bf16[32,192]{1,0:T(8,128)(2,1)S(1)}, u32[]{:S(2)}, u32[]{:S(2)}) collective-permute-start(bf16[32,192]{1,0:T(8,128)(2,1)S(1)} %get-tuple-element.61), channel_id=1, source_target_pairs={{0,2},{1,3},{2,0},{3,1},{4,6},{5,7},{6,4},{7,5},{8,10},{9,11},{10,... | collective-permute-start | bytes 36872 | tf_op jit(solution)/shard_map/ppermute | solution.py:28
  69.7 1.4 %collective-permute-done.20 = bf16[32,192]{1,0:T(8,128)(2,1)S(1)} collective-permute-done((bf16[32,192]{1,0:T(8,128)(2,1)S(1)}, bf16[32,192]{1,0:T(8,128)(2,1)S(1)}, u32[]{:S(2)}, u32[]{:S(2)}) %collective-permute-start.20) | collective-permute-done | bytes 12320 | tf_op jit(solution)/shard_map/ppermute | solution.py:28
  (57 shorter events, 9.9 us)
Async XLA Ops:
  2.5 6.0 %collective-permute-start = (bf16[80,128]{1,0:T(8,128)(2,1)S(1)}, bf16[80,128]{1,0:T(8,128)(2,1)S(1)}, u32[]{:S(2)}, u32[]{:S(2)}) collective-permute-start(bf16[80,128]{1,0:T(8,128)(2,1)S(1)} %get-tuple-element.33.after), channel_id=1, source_target_pairs={{4,8},{12,16},{20,24},{28,32},{36,40},{44,48},{52,56},{60,64},{68,... | collective-permute-start | bytes 61448 | tf_op jit(solution)/shard_map/ppermute | solution.py:33
  4.7 3.9 %collective-permute-start.1 = (bf16[80,128]{1,0:T(8,128)(2,1)S(1)}, bf16[80,128]{1,0:T(8,128)(2,1)S(1)}, u32[]{:S(2)}, u32[]{:S(2)}) collective-permute-start(bf16[80,128]{1,0:T(8,128)(2,1)S(1)} %get-tuple-element.34), channel_id=1, source_target_pairs={{0,4},{8,12},{16,20},{24,28},{32,36},{40,44},{48,52},{56,60},{64,6... | collective-permute-start | bytes 61448 | tf_op jit(solution)/shard_map/ppermute | solution.py:33
  8.6 11.3 %copy-start.1 = (bf16[768,4,192]{0,2,1:T(8,128)(2,1)S(1)}, bf16[768,4,192]{0,2,1:T(8,128)(2,1)}, u32[]{:S(2)}) copy-start(bf16[768,4,192]{0,2,1:T(8,128)(2,1)} %param.20) | copy-start | bytes 3538948
  11.3 5.8 %collective-permute-start.2 = (bf16[32,768]{1,0:T(8,128)(2,1)S(1)}, bf16[32,768]{1,0:T(8,128)(2,1)S(1)}, u32[]{:S(2)}, u32[]{:S(2)}) collective-permute-start(bf16[32,768]{1,0:T(8,128)(2,1)S(1)} %get-tuple-element.41.p0), channel_id=1, source_target_pairs={{0,1},{1,2},{2,3},{3,0},{4,5},{5,6},{6,7},{7,4},{8,9},{9,10},{10,1... | collective-permute-start | bytes 147464 | tf_op jit(solution)/shard_map/ppermute | solution.py:28
  12.9 6.5 %collective-permute-start.3 = (bf16[32,768]{1,0:T(8,128)(2,1)S(1)}, bf16[32,768]{1,0:T(8,128)(2,1)S(1)}, u32[]{:S(2)}, u32[]{:S(2)}) collective-permute-start(bf16[32,768]{1,0:T(8,128)(2,1)S(1)} %get-tuple-element.41.p0), channel_id=1, source_target_pairs={{0,2},{1,3},{2,0},{3,1},{4,6},{5,7},{6,4},{7,5},{8,10},{9,11},{10,... | collective-permute-start | bytes 147464 | tf_op jit(solution)/shard_map/ppermute | solution.py:28
  15.8 4.1 %collective-permute-start.4 = (bf16[32,768]{1,0:T(8,128)(2,1)S(1)}, bf16[32,768]{1,0:T(8,128)(2,1)S(1)}, u32[]{:S(2)}, u32[]{:S(2)}) collective-permute-start(bf16[32,768]{1,0:T(8,128)(2,1)S(1)} %get-tuple-element.41.p0), channel_id=1, source_target_pairs={{0,3},{1,0},{2,1},{3,2},{4,7},{5,4},{6,5},{7,6},{8,11},{9,8},{10,9... | collective-permute-start | bytes 147464 | tf_op jit(solution)/shard_map/ppermute | solution.py:28
  19.9 32.8 %copy-start.3 = (bf16[192,768]{1,0:T(8,128)(2,1)S(1)}, bf16[192,768]{1,0:T(8,128)(2,1)}, u32[]{:S(2)}) copy-start(bf16[192,768]{1,0:T(8,128)(2,1)} %w_out.1) | copy-start | bytes 884740
  21.2 18.6 %all-to-all-start = ((bf16[8,32,384]{2,1,0:T(8,128)(2,1)}), bf16[8,32,384]{2,1,0:T(8,128)(2,1)S(1)}, u32[]{:S(2)}, u32[]{:S(2)}) async-start(bf16[8,32,384]{2,1,0:T(8,128)(2,1)} %get-tuple-element.42), calls=%async_computation | async-start | bytes 393216 | tf_op jit(solution)/shard_map/all_to_all | solution.py:41
  29.0 6.8 %collective-permute-start.5 = (bf16[4,32,512]{2,1,0:T(8,128)(2,1)S(1)}, bf16[4,32,512]{2,1,0:T(8,128)(2,1)S(1)}, u32[]{:S(2)}, u32[]{:S(2)}) collective-permute-start(bf16[4,32,512]{2,1,0:T(8,128)(2,1)S(1)} %get-tuple-element.48), channel_id=1, source_target_pairs={{0,1},{1,2},{2,3},{3,0},{4,5},{5,6},{6,7},{7,4},{8,9},{9,10},{10,1... | collective-permute-start | bytes 393224 | tf_op jit(solution)/shard_map/ppermute | solution.py:28
  29.3 9.8 %collective-permute-start.6 = (bf16[4,32,512]{2,1,0:T(8,128)(2,1)S(1)}, bf16[4,32,512]{2,1,0:T(8,128)(2,1)S(1)}, u32[]{:S(2)}, u32[]{:S(2)}) collective-permute-start(bf16[4,32,512]{2,1,0:T(8,128)(2,1)S(1)} %get-tuple-element.49), channel_id=1, source_target_pairs={{0,2},{1,3},{2,0},{3,1},{4,6},{5,7},{6,4},{7,5},{8,10},{9,11},{10,... | collective-permute-start | bytes 393224 | tf_op jit(solution)/shard_map/ppermute | solution.py:28
  33.0 6.1 %collective-permute-start.7 = (bf16[4,32,512]{2,1,0:T(8,128)(2,1)S(1)}, bf16[4,32,512]{2,1,0:T(8,128)(2,1)S(1)}, u32[]{:S(2)}, u32[]{:S(2)}) collective-permute-start(bf16[4,32,512]{2,1,0:T(8,128)(2,1)S(1)} %get-tuple-element.50), channel_id=1, source_target_pairs={{0,3},{1,0},{2,1},{3,2},{4,7},{5,4},{6,5},{7,6},{8,11},{9,8},{10,9... | collective-permute-start | bytes 393224 | tf_op jit(solution)/shard_map/ppermute | solution.py:28
  39.8 9.1 %collective-permute-start.8 = (bf16[8,32,384]{2,1,0:T(8,128)(2,1)S(1)}, bf16[8,32,384]{2,1,0:T(8,128)(2,1)S(1)}, u32[]{:S(2)}, u32[]{:S(2)}) collective-permute-start(bf16[8,32,384]{2,1,0:T(8,128)(2,1)S(1)} %all-to-all-done.own0), channel_id=1, source_target_pairs={{0,8},{8,16},{16,24},{24,0},{1,9},{9,17},{17,25},{25,1},{2,10},{10... | collective-permute-start | bytes 589832 | tf_op jit(solution)/shard_map/ppermute | solution.py:28
  42.3 7.3 %collective-permute-start.9 = (bf16[8,32,384]{2,1,0:T(8,128)(2,1)S(1)}, bf16[8,32,384]{2,1,0:T(8,128)(2,1)S(1)}, u32[]{:S(2)}, u32[]{:S(2)}) collective-permute-start(bf16[8,32,384]{2,1,0:T(8,128)(2,1)S(1)} %all-to-all-done.own0), channel_id=1, source_target_pairs={{0,16},{8,24},{16,0},{24,8},{1,17},{9,25},{17,1},{25,9},{2,18},{10... | collective-permute-start | bytes 589832 | tf_op jit(solution)/shard_map/ppermute | solution.py:28
  42.3 9.0 %collective-permute-start.10 = (bf16[8,32,384]{2,1,0:T(8,128)(2,1)S(1)}, bf16[8,32,384]{2,1,0:T(8,128)(2,1)S(1)}, u32[]{:S(2)}, u32[]{:S(2)}) collective-permute-start(bf16[8,32,384]{2,1,0:T(8,128)(2,1)S(1)} %all-to-all-done.own0), channel_id=1, source_target_pairs={{0,24},{8,0},{16,8},{24,16},{1,25},{9,1},{17,9},{25,17},{2,26},{10... | collective-permute-start | bytes 589832 | tf_op jit(solution)/shard_map/ppermute | solution.py:28
  43.2 8.1 %collective-permute-start.11 = (bf16[8,32,384]{2,1,0:T(8,128)(2,1)S(1)}, bf16[8,32,384]{2,1,0:T(8,128)(2,1)S(1)}, u32[]{:S(2)}, u32[]{:S(2)}) collective-permute-start(bf16[8,32,384]{2,1,0:T(8,128)(2,1)S(1)} %all-to-all-done.own0), channel_id=1, source_target_pairs={{0,4},{4,0},{1,5},{5,1},{2,6},{6,2},{3,7},{7,3},{8,12},{12,8},{9,1... | collective-permute-start | bytes 589832 | tf_op jit(solution)/shard_map/ppermute | solution.py:28
  48.9 2.4 %collective-permute-start.12 = (bf16[8,32,384]{2,1,0:T(8,128)(2,1)S(1)}, bf16[8,32,384]{2,1,0:T(8,128)(2,1)S(1)}, u32[]{:S(2)}, u32[]{:S(2)}) collective-permute-start(bf16[8,32,384]{2,1,0:T(8,128)(2,1)S(1)} %collective-permute-done.8.own1), channel_id=1, source_target_pairs={{0,4},{4,0},{1,5},{5,1},{2,6},{6,2},{3,7},{7,3},{8,12},{12,8},{9,1... | collective-permute-start | bytes 589832 | tf_op jit(solution)/shard_map/ppermute | solution.py:28
  49.6 1.7 %collective-permute-start.13 = (bf16[8,32,384]{2,1,0:T(8,128)(2,1)S(1)}, bf16[8,32,384]{2,1,0:T(8,128)(2,1)S(1)}, u32[]{:S(2)}, u32[]{:S(2)}) collective-permute-start(bf16[8,32,384]{2,1,0:T(8,128)(2,1)S(1)} %collective-permute-done.9.own2), channel_id=1, source_target_pairs={{0,4},{4,0},{1,5},{5,1},{2,6},{6,2},{3,7},{7,3},{8,12},{12,8},{9,1... | collective-permute-start | bytes 589832 | tf_op jit(solution)/shard_map/ppermute | solution.py:28
  51.3 1.4 %collective-permute-start.14 = (bf16[8,32,384]{2,1,0:T(8,128)(2,1)S(1)}, bf16[8,32,384]{2,1,0:T(8,128)(2,1)S(1)}, u32[]{:S(2)}, u32[]{:S(2)}) collective-permute-start(bf16[8,32,384]{2,1,0:T(8,128)(2,1)S(1)} %collective-permute-done.10.own3), channel_id=1, source_target_pairs={{0,4},{4,0},{1,5},{5,1},{2,6},{6,2},{3,7},{7,3},{8,12},{12,8},{9,1... | collective-permute-start | bytes 589832 | tf_op jit(solution)/shard_map/ppermute | solution.py:28
  54.6 5.4 %collective-permute-start.15 = (bf16[32,768]{1,0:T(8,128)(2,1)S(1)}, bf16[32,768]{1,0:T(8,128)(2,1)S(1)}, u32[]{:S(2)}, u32[]{:S(2)}) collective-permute-start(bf16[32,768]{1,0:T(8,128)(2,1)S(1)} %shard_map.144.p0), channel_id=1, source_target_pairs={{0,1},{1,2},{2,3},{3,0},{4,5},{5,6},{6,7},{7,4},{8,9},{9,10},{10,1... | collective-permute-start | bytes 147464 | tf_op jit(solution)/shard_map/ppermute | solution.py:28
  56.5 5.6 %collective-permute-start.16 = (bf16[32,768]{1,0:T(8,128)(2,1)S(1)}, bf16[32,768]{1,0:T(8,128)(2,1)S(1)}, u32[]{:S(2)}, u32[]{:S(2)}) collective-permute-start(bf16[32,768]{1,0:T(8,128)(2,1)S(1)} %shard_map.144.p0), channel_id=1, source_target_pairs={{0,2},{1,3},{2,0},{3,1},{4,6},{5,7},{6,4},{7,5},{8,10},{9,11},{10,... | collective-permute-start | bytes 147464 | tf_op jit(solution)/shard_map/ppermute | solution.py:28
  58.9 4.1 %collective-permute-start.17 = (bf16[32,768]{1,0:T(8,128)(2,1)S(1)}, bf16[32,768]{1,0:T(8,128)(2,1)S(1)}, u32[]{:S(2)}, u32[]{:S(2)}) collective-permute-start(bf16[32,768]{1,0:T(8,128)(2,1)S(1)} %shard_map.144.p0), channel_id=1, source_target_pairs={{0,3},{1,0},{2,1},{3,2},{4,7},{5,4},{6,5},{7,6},{8,11},{9,8},{10,9... | collective-permute-start | bytes 147464 | tf_op jit(solution)/shard_map/ppermute | solution.py:28
  64.3 5.0 %collective-permute-start.18 = (bf16[32,192]{1,0:T(8,128)(2,1)S(1)}, bf16[32,192]{1,0:T(8,128)(2,1)S(1)}, u32[]{:S(2)}, u32[]{:S(2)}) collective-permute-start(bf16[32,192]{1,0:T(8,128)(2,1)S(1)} %get-tuple-element.60), channel_id=1, source_target_pairs={{0,1},{1,2},{2,3},{3,0},{4,5},{5,6},{6,7},{7,4},{8,9},{9,10},{10,1... | collective-permute-start | bytes 36872 | tf_op jit(solution)/shard_map/ppermute | solution.py:28
  64.4 5.2 %collective-permute-start.19 = (bf16[32,192]{1,0:T(8,128)(2,1)S(1)}, bf16[32,192]{1,0:T(8,128)(2,1)S(1)}, u32[]{:S(2)}, u32[]{:S(2)}) collective-permute-start(bf16[32,192]{1,0:T(8,128)(2,1)S(1)} %get-tuple-element.61), channel_id=1, source_target_pairs={{0,2},{1,3},{2,0},{3,1},{4,6},{5,7},{6,4},{7,5},{8,10},{9,11},{10,... | collective-permute-start | bytes 36872 | tf_op jit(solution)/shard_map/ppermute | solution.py:28
  67.4 3.7 %collective-permute-start.20 = (bf16[32,192]{1,0:T(8,128)(2,1)S(1)}, bf16[32,192]{1,0:T(8,128)(2,1)S(1)}, u32[]{:S(2)}, u32[]{:S(2)}) collective-permute-start(bf16[32,192]{1,0:T(8,128)(2,1)S(1)} %get-tuple-element.62), channel_id=1, source_target_pairs={{0,3},{1,0},{2,1},{3,2},{4,7},{5,4},{6,5},{7,6},{8,11},{9,8},{10,9... | collective-permute-start | bytes 36872 | tf_op jit(solution)/shard_map/ppermute | solution.py:28
  (11 other events, 59.4 us)
